TPU v7x, 32 devices: a whole 2x2x4 slice. The times are simulated.
32 devices in a mesh: pix: 8 (over z, y), ch: 4 (over x, core).
Axes of the slice: x: 2, y: 2, z: 4, core: 2. Of those that a mesh axis runs over, the one named last changes fastest.
Arguments:
- features: bfloat16 [64, 128, 2048], P('pix', None, 'ch'), may hold values from -6 to 6
- pixel_mask: int32 [64, 128], P('pix'), may hold values from 0 to 1, as said below
- reduce_weight: bfloat16 [2048, 512], P(None, 'ch'), may hold values from -0.125 to 0.125
- reduce_gain: float32 [512], P('ch'), may hold values from 0.5 to 1.5
- reduce_bias: float32 [512], P('ch'), may hold values from -1.5 to 1.5
- dilated_weight: bfloat16 [3, 3, 512, 512], P(None, None, 'ch'), may hold values from -0.09375 to 0.09375
- dilated_gain: float32 [512], P('ch'), may hold values from 0.5 to 1.5
- dilated_bias: float32 [512], P('ch'), may hold values from -1.5 to 1.5
- expand_weight: bfloat16 [512, 2048], P('ch'), may hold values from -0.25 to 0.25
- expand_gain: float32 [2048], P('ch'), may hold values from 0.5 to 1.5
- expand_bias: float32 [2048], P('ch'), may hold values from -1.5 to 1.5
- aspp_weight: bfloat16 [3, 3, 3, 2048, 256], P(None, None, None, 'ch'), may hold values from -0.046875 to 0.046875
- aspp_gain: float32 [3, 256], P(None, 'ch'), may hold values from 0.5 to 1.5
- aspp_bias: float32 [3, 256], P(None, 'ch'), may hold values from -1.5 to 1.5
- task_weight: bfloat16 [3, 256, 23], P(None, 'ch'), may hold values from -0.21875 to 0.21875
- cotangent: float32 [64, 128, 23], P('pix'), may hold values from -24 to 24
Outputs:
- predictions: float32 [64, 128, 23], P('pix')
- features_grad: bfloat16 [64, 128, 2048], P('pix', None, 'ch')
- reduce_weight_grad: float32 [2048, 512], P('pix', 'ch')
- reduce_gain_grad: float32 [512], P('ch')
- reduce_bias_grad: float32 [512], P('ch')
- dilated_weight_grad: float32 [3, 3, 512, 512], P(None, None, 'ch', 'pix')
- dilated_gain_grad: float32 [512], P('ch')
- dilated_bias_grad: float32 [512], P('ch')
- expand_weight_grad: float32 [512, 2048], P('ch', 'pix')
- expand_gain_grad: float32 [2048], P('ch')
- expand_bias_grad: float32 [2048], P('ch')
- aspp_weight_grad: float32 [3, 3, 3, 2048, 256], P(None, None, None, 'ch', 'pix')
- aspp_gain_grad: float32 [3, 256], P(None, 'ch')
- aspp_bias_grad: float32 [3, 256], P(None, 'ch')
- task_weight_grad: float32 [3, 256, 23], P(None, 'ch')
Inputs may be any that keep to these rules, and one draw needn't show every extreme that they name: `pixel_mask`: each row holds padding; the share of image pixels rises from about 0.3 in the first rows to about 0.9 in the last.
All inputs are finite; a program needn't handle non-finite values.
Results may differ from a plain program's by a relative error of at most 0.025.
Values may be sent and summed in bfloat16 or wider, within the bound.
A program may use at most 256 MiB of HBM per device.

v0:
```python
import jax
import jax.numpy as jnp
from jax import lax
from jax.sharding import PartitionSpec as P

CLS = 19


epsilon = 1e-05
highest = lax.Precision.HIGHEST
aspp_rates = (12, 24, 36)
inner_rate = 2


def from_behind(value, axis, steps):
    count = lax.axis_size(axis)
    first, last = (max(0, -steps), min(count, count - steps))
    return lax.ppermute(value, axis, [(source, source + steps) for source in range(first, last)])


def with_halo(shard, sides, width):
    for axis, dim in sides:
        devices, length = (lax.axis_size(axis), shard.shape[dim])
        up = [(i, (i + 1) % devices) for i in range(devices - 1)]
        down = [(j, i) for i, j in up]
        last = lax.slice_in_dim(shard, length - width, length, axis=dim)
        first = lax.slice_in_dim(shard, 0, width, axis=dim)
        before = lax.ppermute(last, axis, up)
        after = lax.ppermute(first, axis, down)
        shard = jnp.concatenate([before, shard, after], axis=dim)
    return shard


def silu_slope(value):
    sigma = jax.nn.sigmoid(value)
    return sigma * (1.0 + value * (1.0 - sigma))


def shift_cols(value, offset):
    if offset == 0:
        return value
    margin = abs(offset)
    widths = [(0, 0)] * value.ndim
    widths[1] = (margin, margin)
    padded = jnp.pad(value, widths)
    return lax.slice_in_dim(padded, margin + offset, margin + offset + value.shape[1], axis=1)


def moved(piece, distance):
    return from_behind(piece, "pix", -distance)


def shift_rows(value, offset):
    if offset == 0:
        return value
    steps_over, inner = divmod(offset, value.shape[0])
    first = moved(value, steps_over)[inner:]
    if inner == 0:
        return first
    second = moved(value, steps_over + 1)[:inner]
    return jnp.concatenate([first, second], axis=0)


def halo_rows(value):
    return with_halo(value, (("pix", 0),), inner_rate)


def gather_channels(value):
    return lax.all_gather(value, "ch", axis=1, tiled=True)


def sum_channels(value):
    return lax.psum_scatter(
        value.astype(jnp.bfloat16), "ch", scatter_dimension=1, tiled=True
    ).astype(jnp.float32)


def normalized(hidden, valid, axes):
    total, count = lax.psum(
        (jnp.sum(hidden * valid, axis=axes, keepdims=True), jnp.sum(valid)), "pix"
    )
    center = total / count
    spread_sum = lax.psum(jnp.sum(valid * (hidden - center) ** 2, axis=axes, keepdims=True), "pix")
    variance = spread_sum / count
    scale = lax.rsqrt(variance + epsilon)
    return ((hidden - center) * scale, scale, count)


def norm_grad(grad_out, centered, scale, gain, count, valid, axes):
    sum_out, sum_cross = lax.psum(
        (
            jnp.sum(grad_out, axis=axes, keepdims=True),
            jnp.sum(grad_out * centered, axis=axes, keepdims=True),
        ),
        "pix",
    )
    grad_in = gain * scale * (grad_out - valid * (sum_out + centered * sum_cross) / count)
    return (grad_in, sum_cross, sum_out)


def task_scales(gram):
    norms = jnp.sqrt(jnp.diagonal(gram) + 1e-06)
    proj = gram / norms[None, :]
    vector = proj[0, 0] - proj[0, 1:]
    matrix = proj[0, 0] - proj[0, 1:][None, :] - proj[1:, 0][:, None] + proj[1:, 1:]
    determinant = matrix[0, 0] * matrix[1, 1] - matrix[0, 1] * matrix[1, 0]
    second = (vector[0] * matrix[1, 1] - vector[1] * matrix[1, 0]) / determinant
    third = (vector[1] * matrix[0, 0] - vector[0] * matrix[0, 1]) / determinant
    return jnp.stack([1.0 - second - third, second, third])


def on_device(
    features,
    pixel_mask,
    reduce_weight,
    reduce_gain,
    reduce_bias,
    dilated_weight,
    dilated_gain,
    dilated_bias,
    expand_weight,
    expand_gain,
    expand_bias,
    aspp_weight,
    aspp_gain,
    aspp_bias,
    task_weight,
    cotangent,
):
    rows_here, width, local_in = features.shape
    pixels = rows_here * width
    local_mid = reduce_weight.shape[1]
    full_mid = dilated_weight.shape[3]
    branch_width = aspp_weight.shape[4]
    outs_count = task_weight.shape[2]
    valid = pixel_mask.astype(jnp.float32).reshape(pixels, 1)
    valid_branch = valid[None]
    masked = features.reshape(pixels, local_in) * valid.astype(jnp.bfloat16)
    inputs_full = gather_channels(masked)
    hidden_one = jnp.dot(inputs_full, reduce_weight, preferred_element_type=jnp.float32)
    norm_one, scale_one, count = normalized(hidden_one, valid, (0,))
    pre_one = norm_one * reduce_gain + reduce_bias
    act_one = (jax.nn.silu(pre_one) * valid).astype(jnp.bfloat16)
    padded_one = halo_rows(act_one.reshape(rows_here, width, local_mid))
    partial_value = jnp.zeros((pixels, full_mid), jnp.float32)
    for a in range(3):
        for b in range(3):
            shifted = shift_cols(padded_one[2 * a : 2 * a + rows_here], (b - 1) * inner_rate)
            partial_value = partial_value + jnp.dot(
                shifted.reshape(pixels, local_mid),
                dilated_weight[a, b],
                preferred_element_type=jnp.float32,
            )
    hidden_two = sum_channels(partial_value)
    norm_two, scale_two, _ = normalized(hidden_two, valid, (0,))
    pre_two = norm_two * dilated_gain + dilated_bias
    act_two = (jax.nn.silu(pre_two) * valid).astype(jnp.bfloat16)
    hidden_three = sum_channels(jnp.dot(act_two, expand_weight, preferred_element_type=jnp.float32))
    norm_three, scale_three, _ = normalized(hidden_three, valid, (0,))
    pre_three = norm_three * expand_gain + expand_bias + masked.astype(jnp.float32)
    trunk_out = (
        (jax.nn.silu(pre_three) * valid).astype(jnp.bfloat16).reshape(rows_here, width, local_in)
    )
    kept_rows = []
    partials = []
    for j in range(3):
        rate = aspp_rates[j]
        running = jnp.zeros((pixels, branch_width), jnp.float32)
        shifted_rows = []
        for a in range(3):
            row_shift = shift_rows(trunk_out, (a - 1) * rate)
            shifted_rows.append(row_shift)
            for b in range(3):
                shifted = shift_cols(row_shift, (b - 1) * rate)
                running = running + jnp.dot(
                    shifted.reshape(pixels, local_in),
                    aspp_weight[j, a, b],
                    preferred_element_type=jnp.float32,
                )
        kept_rows.append(shifted_rows)
        partials.append(running)
    branch_sum = sum_channels(jnp.stack(partials).reshape(3 * pixels, branch_width)).reshape(
        3, pixels, -1
    )
    branch_gain = aspp_gain[:, None, :]
    norm_branch, scale_branch, _ = normalized(branch_sum, valid_branch, (1,))
    pre_branch = norm_branch * branch_gain + aspp_bias[:, None, :]
    branch_out = (jax.nn.silu(pre_branch) * valid_branch).astype(jnp.bfloat16)
    predictions = lax.psum(
        jnp.einsum(
            "jpc,jco->po", branch_out, task_weight, preferred_element_type=jnp.float32
        ).astype(jnp.bfloat16),
        "ch",
    ).astype(jnp.float32)
    columns = jnp.arange(outs_count)
    task_of = (columns >= CLS).astype(jnp.int32) + (columns >= CLS + 1).astype(jnp.int32)
    select = (task_of[:, None] == jnp.arange(3)[None, :]).astype(jnp.float32)
    target = cotangent.reshape(pixels, outs_count) * valid
    task_float = task_weight.astype(jnp.float32)
    task_grads = jnp.einsum("po,ot,jco->tjpc", target, select, task_float, precision=highest)
    gram = lax.psum(
        jnp.einsum("tjpc,sjpc->ts", task_grads, task_grads, precision=highest), ("pix", "ch")
    )
    scales = task_scales(gram)
    branch_grad = jnp.einsum("t,tjpc->jpc", scales, task_grads, precision=highest)
    task_weight_grad = lax.psum(
        jnp.einsum("jpc,po->jco", branch_out.astype(jnp.float32), target, precision=highest), "pix"
    )
    grad_pre_branch = branch_grad * valid_branch * silu_slope(pre_branch)
    grad_branch, aspp_gain_grad, aspp_bias_grad = norm_grad(
        grad_pre_branch, norm_branch, scale_branch, branch_gain, count, valid_branch, (1,)
    )
    grad_full = gather_channels(grad_branch.astype(jnp.bfloat16).reshape(3 * pixels, -1)).reshape(
        3, rows_here, width, -1
    )
    grad_trunk = jnp.zeros((pixels, local_in), jnp.float32)
    aspp_list = []
    for j in range(3):
        rate = aspp_rates[j]
        grad_flat = grad_full[j].reshape(pixels, -1)
        per_row = []
        for a in range(3):
            back_rows = shift_rows(grad_full[j], -(a - 1) * rate)
            per_col = []
            for b in range(3):
                shifted = shift_cols(back_rows, -(b - 1) * rate)
                grad_trunk = grad_trunk + jnp.einsum(
                    "pa,ca->pc",
                    shifted.reshape(pixels, -1),
                    aspp_weight[j, a, b],
                    preferred_element_type=jnp.float32,
                )
                forward_tap = shift_cols(kept_rows[j][a], (b - 1) * rate).reshape(pixels, local_in)
                per_col.append(
                    jnp.einsum(
                        "pc,pa->ca", forward_tap, grad_flat, preferred_element_type=jnp.float32
                    )
                )
            per_row.append(jnp.stack(per_col))
        aspp_list.append(jnp.stack(per_row))
    aspp_weight_local = jnp.stack(aspp_list)
    grad_pre_three = grad_trunk * valid * silu_slope(pre_three)
    grad_three, expand_gain_grad, expand_bias_grad = norm_grad(
        grad_pre_three, norm_three, scale_three, expand_gain, count, valid, (0,)
    )
    grad_three_full = gather_channels(grad_three.astype(jnp.bfloat16))
    grad_act_two = jnp.einsum(
        "pc,dc->pd", grad_three_full, expand_weight, preferred_element_type=jnp.float32
    )
    expand_weight_local = jnp.einsum(
        "pd,pc->dc", act_two, grad_three_full, preferred_element_type=jnp.float32
    )
    grad_pre_two = grad_act_two * valid * silu_slope(pre_two)
    grad_two, dilated_gain_grad, dilated_bias_grad = norm_grad(
        grad_pre_two, norm_two, scale_two, dilated_gain, count, valid, (0,)
    )
    grad_two_full = gather_channels(grad_two.astype(jnp.bfloat16))
    padded_grad = halo_rows(grad_two_full.reshape(rows_here, width, full_mid))
    grad_act_one = jnp.zeros((pixels, local_mid), jnp.float32)
    dilated_rows = []
    for a in range(3):
        dilated_cols = []
        for b in range(3):
            shifted = shift_cols(
                padded_grad[4 - 2 * a : 4 - 2 * a + rows_here], -(b - 1) * inner_rate
            )
            grad_act_one = grad_act_one + jnp.einsum(
                "pe,de->pd",
                shifted.reshape(pixels, full_mid),
                dilated_weight[a, b],
                preferred_element_type=jnp.float32,
            )
            forward_tap = shift_cols(
                padded_one[2 * a : 2 * a + rows_here], (b - 1) * inner_rate
            ).reshape(pixels, local_mid)
            dilated_cols.append(
                jnp.einsum(
                    "pd,pe->de", forward_tap, grad_two_full, preferred_element_type=jnp.float32
                )
            )
        dilated_rows.append(jnp.stack(dilated_cols))
    dilated_weight_local = jnp.stack(dilated_rows)
    grad_pre_one = grad_act_one * valid * silu_slope(pre_one)
    grad_one, reduce_gain_grad, reduce_bias_grad = norm_grad(
        grad_pre_one, norm_one, scale_one, reduce_gain, count, valid, (0,)
    )
    grad_one_low = grad_one.astype(jnp.bfloat16)
    input_sum = sum_channels(
        jnp.einsum("pd,cd->pc", grad_one_low, reduce_weight, preferred_element_type=jnp.float32)
    )
    features_grad = (
        ((input_sum + grad_pre_three) * valid)
        .astype(jnp.bfloat16)
        .reshape(rows_here, width, local_in)
    )
    reduce_weight_local = jnp.einsum(
        "pc,pd->cd", inputs_full, grad_one_low, preferred_element_type=jnp.float32
    )
    reduce_weight_grad, dilated_weight_grad, expand_weight_grad, aspp_weight_grad = (
        lax.psum_scatter(reduce_weight_local, "pix", scatter_dimension=0, tiled=True),
        lax.psum_scatter(dilated_weight_local, "pix", scatter_dimension=3, tiled=True),
        lax.psum_scatter(expand_weight_local, "pix", scatter_dimension=1, tiled=True),
        lax.psum_scatter(aspp_weight_local, "pix", scatter_dimension=4, tiled=True),
    )
    return (
        predictions.reshape(rows_here, width, outs_count),
        features_grad,
        reduce_weight_grad,
        reduce_gain_grad.reshape(-1),
        reduce_bias_grad.reshape(-1),
        dilated_weight_grad,
        dilated_gain_grad.reshape(-1),
        dilated_bias_grad.reshape(-1),
        expand_weight_grad,
        expand_gain_grad.reshape(-1),
        expand_bias_grad.reshape(-1),
        aspp_weight_grad,
        aspp_gain_grad.reshape(3, -1),
        aspp_bias_grad.reshape(3, -1),
        task_weight_grad,
    )


def solution(mesh):
    placed = (
        P("pix", None, "ch"),
        P("pix", None),
        P(None, "ch"),
        P("ch"),
        P("ch"),
        P(None, None, "ch", None),
        P("ch"),
        P("ch"),
        P("ch", None),
        P("ch"),
        P("ch"),
        P(None, None, None, "ch", None),
        P(None, "ch"),
        P(None, "ch"),
        P(None, "ch", None),
        P("pix", None, None),
    )
    return jax.shard_map(
        on_device,
        mesh=mesh,
        in_specs=placed,
        out_specs=(
            P("pix", None, None),
            P("pix", None, "ch"),
            P("pix", "ch"),
            P("ch"),
            P("ch"),
            P(None, None, "ch", "pix"),
            P("ch"),
            P("ch"),
            P("ch", "pix"),
            P("ch"),
            P("ch"),
            P(None, None, None, "ch", "pix"),
            P(None, "ch"),
            P(None, "ch"),
            P(None, "ch", None),
        ),
        check_vma=False,
    )
```

profile of v0, /device:TPU:0, one launch (start us, length us, event | category | flops | bytes accessed | tf_op | source)
XLA Modules:
  0.0 1850.2 jit_solution(12466093364100718978)
XLA Ops:
  8.6 2.4 bitcast_multiply_fusion.1
  11.7 36.7 %all-gather.5.cloned.1.call-done = bf16[1024,2048]{1,0:T(8,128)(2,1)} async-done(((bf16[1024,512]{1,0:T(8,128)(2,1)}), bf16[1024,2048]{1,0:T(8,128)(2,1)}) %all-gather.5.cloned.1.call-update) | async-done | bytes 4194320 | tf_op jit(solution)/shard_map/all_gather | solution.py:69
  48.4 3.5 multiply_reduce_fusion.5
  51.9 22.0 %all-reduce.30 = (f32[1,128]{1,0:T(1,128)S(1)}, f32[]{:T(128)}) all-reduce(f32[1,128]{1,0:T(1,128)S(1)} %bitcast.904, f32[]{:T(128)} %convert_reduce_fusion), channel_id=1, replica_groups=mesh['pix'=8,'ch'=4] {'pix'}, use_global_device_ids=true, to_apply=%region_1.0 | all-reduce | flops 129 | bytes 1032 | tf_op jit(solution)/shard_map/psum | solution.py:79
  74.8 17.2 psum.151
  95.1 4.5 collective-permute-start
  107.4 25.4 %reduce-scatter.19.cloned.1.call-done = bf16[128,1024]{1,0:T(8,128)(2,1)} async-done(((bf16[512,1024]{1,0:T(8,128)(2,1)}), bf16[128,1024]{1,0:T(8,128)(2,1)}) %reduce-scatter.19.cloned.1.call-update) | async-done | bytes 262160
  134.1 21.4 %psum.152 = f32[1,128]{1,0:T(1,128)S(1)} all-reduce(f32[1,128]{1,0:T(1,128)S(1)} %bitcast.901), channel_id=1, replica_groups=mesh['pix'=8,'ch'=4] {'pix'}, use_global_device_ids=true, to_apply=%region_8.9 | all-reduce | flops 128 | bytes 1024 | tf_op jit(solution)/shard_map/psum | solution.py:79
  156.3 17.1 psum.153
  174.7 3.3 convolution_convert_fusion.1
  178.1 42.4 %reduce-scatter.9.cloned.1.call-done = bf16[1024,512]{1,0:T(8,128)(2,1)} async-done(((bf16[1024,2048]{1,0:T(8,128)(2,1)}), bf16[1024,512]{1,0:T(8,128)(2,1)}) %reduce-scatter.9.cloned.1.call-update) | async-done | bytes 1048592 | tf_op jit(solution)/shard_map/reduce_scatter | solution.py:73
  222.0 21.4 %psum.154 = f32[1,512]{1,0:T(1,128)S(1)} all-reduce(f32[1,512]{1,0:T(1,128)S(1)} %bitcast.892), channel_id=1, replica_groups=mesh['pix'=8,'ch'=4] {'pix'}, use_global_device_ids=true, to_apply=%region_13.14 | all-reduce | flops 512 | bytes 4096 | tf_op jit(solution)/shard_map/psum | solution.py:79
  245.6 17.1 psum.155
  264.0 2.7 multiply_convert_fusion.1
  269.4 4.0 collective-permute-start.3
  276.0 58.0 %collective-permute-done.11 = bf16[8,128,512]{2,1,0:T(8,128)(2,1)S(1)} collective-permute-done((bf16[8,128,512]{2,1,0:T(8,128)(2,1)S(1)}, bf16[8,128,512]{2,1,0:T(8,128)(2,1)S(1)}, u32[]{:S(2)}, u32[]{:S(2)}) %collective-permute-start.11) | collective-permute-done | bytes 1048608 | tf_op jit(solution)/shard_map/ppermute | solution.py:18
  339.1 24.9 %collective-permute-start.9 = (bf16[8,128,512]{2,1,0:T(8,128)(2,1)S(1)}, bf16[8,128,512]{2,1,0:T(8,128)(2,1)S(1)}, u32[]{:S(2)}, u32[]{:S(2)}) collective-permute-start(bf16[8,128,512]{2,1,0:T(8,128)(2,1)S(1)} %bitcast.744), channel_id=1, source_target_pairs={{0,16},{4,20},{8,24},{12,28},{1,17},{5,21},{9,25},{13,29},{2,18},{... | collective-permute-start | bytes 3145736 | tf_op jit(solution)/shard_map/ppermute | solution.py:18
  366.6 13.9 collective-permute-start.8
  381.5 37.9 %collective-permute-done.6 = bf16[8,128,512]{2,1,0:T(8,128)(2,1)S(1)} collective-permute-done((bf16[8,128,512]{2,1,0:T(8,128)(2,1)S(1)}, bf16[8,128,512]{2,1,0:T(8,128)(2,1)S(1)}, u32[]{:S(2)}, u32[]{:S(2)}) %collective-permute-start.6) | collective-permute-done | bytes 1048608 | tf_op jit(solution)/shard_map/ppermute | solution.py:18
  423.3 11.9 collective-permute-done.8
  449.9 13.8 fusion.36
  463.7 59.9 %psum.159 = f32[3,3]{1,0:T(4,128)S(1)} all-reduce(f32[3,3]{1,0:T(4,128)S(1)} %fusion.36), channel_id=1, replica_groups=mesh['pix'=8,'ch'=4] {'pix','ch'}, use_global_device_ids=true, to_apply=%region_22.23 | all-reduce | flops 9 | bytes 72 | tf_op jit(solution)/shard_map/psum | solution.py:201
  535.1 7.1 fusion
  544.3 36.1 %psum.156 = f32[3,1,64]{0,2,1:T(8,128)S(1)} all-reduce(f32[3,1,64]{0,2,1:T(8,128)S(1)} %bitcast.878), channel_id=1, replica_groups=mesh['pix'=8,'ch'=4] {'pix'}, use_global_device_ids=true, to_apply=%region_18.19 | all-reduce | flops 192 | bytes 1536 | tf_op jit(solution)/shard_map/psum | solution.py:79
  581.5 33.0 %psum.157 = f32[3,1,64]{0,2,1:T(8,128)S(1)} all-reduce(f32[3,1,64]{0,2,1:T(8,128)S(1)} %bitcast.879), channel_id=1, replica_groups=mesh['pix'=8,'ch'=4] {'pix'}, use_global_device_ids=true, to_apply=%region_20.21 | all-reduce | flops 192 | bytes 1536 | tf_op jit(solution)/shard_map/psum | solution.py:83
  615.8 2.9 fusion.357
  618.7 34.0 %all-reduce.29 = (f32[3,64]{0,1:T(8,128)}, f32[3,64]{0,1:T(8,128)}) all-reduce(f32[3,64]{0,1:T(8,128)S(1)} %get-tuple-element.63, f32[3,64]{0,1:T(8,128)S(1)} %get-tuple-element.62), channel_id=1, replica_groups=mesh['pix'=8,'ch'=4] {'pix'}, use_global_device_ids=true, to_apply=%region_26.27 | all-reduce | flops 384 | bytes 3072 | tf_op jit(solution)/shard_map/psum | solution.py:90
  652.7 4.1 multiply_convert_fusion.2
  657.8 17.6 all-gather.7.cloned.1.call-done
  677.0 4.6 collective-permute-start.21
  681.6 2.2 collective-permute-start.20
  686.9 3.4 collective-permute-start.15
  708.3 16.6 collective-permute-done.19
  724.9 9.1 collective-permute-start.14
  735.9 3.5 collective-permute-start.17
  742.6 3.6 collective-permute-done.14
  747.7 19.5 %collective-permute-done.17 = bf16[8,128,256]{1,0,2:T(8,128)(2,1)S(1)} collective-permute-done((bf16[8,128,256]{1,0,2:T(8,128)(2,1)S(1)}, bf16[8,128,256]{1,0,2:T(8,128)(2,1)S(1)}, u32[]{:S(2)}, u32[]{:S(2)}) %collective-permute-start.17) | collective-permute-done | bytes 524320 | tf_op jit(solution)/shard_map/ppermute | solution.py:18
  798.8 21.6 %fusion.356 = (f32[512]{0:T(512)S(1)}, f32[512]{0:T(512)S(1)}, f32[1024,512]{1,0:T(8,128)}) fusion(f32[512]{0:T(512)S(1)} %bitcast.888, f32[512]{0:T(512)S(1)} %bitcast.884, bf16[1024,512]{1,0:T(8,128)(2,1)} %reduce-scatter.9.cloned.1.call-done, bf16[1024,512]{1,0:T(8,128)(2,1)} %bitcast_multiply_fusion.1, f32[512]{0:T(512)} %param.26, ...), kind=kOutput, calls=%fused_computation.560 | convolution fusion | flops 292027392 | bytes 59523072 | tf_op jit(solution)/shard_map/pa,ca->pc/dot_general | solution.py:227
  820.5 24.5 %all-reduce.28 = (f32[512]{0:T(512)S(1)}, f32[512]{0:T(512)S(1)}) all-reduce(f32[512]{0:T(512)S(1)} %get-tuple-element.61, f32[512]{0:T(512)S(1)} %get-tuple-element.60), channel_id=1, replica_groups=mesh['pix'=8,'ch'=4] {'pix'}, use_global_device_ids=true, to_apply=%region_30.31 | all-reduce | flops 1024 | bytes 8192 | tf_op jit(solution)/shard_map/psum | solution.py:90
  845.0 3.9 fusion.20
  852.8 27.2 %all-gather.9.cloned.1.call-done = bf16[1024,2048]{1,0:T(8,128)(2,1)} async-done(((bf16[1024,512]{1,0:T(8,128)(2,1)}), bf16[1024,2048]{1,0:T(8,128)(2,1)}) %all-gather.9.cloned.1.call-update) | async-done | bytes 4194320 | tf_op jit(solution)/shard_map/all_gather | solution.py:69
  880.0 4.3 fusion.359
  884.3 21.5 %all-reduce.27 = (f32[128]{0:T(128)S(1)}, f32[128]{0:T(128)S(1)}) all-reduce(f32[128]{0:T(128)S(1)} %get-tuple-element.67, f32[128]{0:T(128)S(1)} %get-tuple-element.66), channel_id=1, replica_groups=mesh['pix'=8,'ch'=4] {'pix'}, use_global_device_ids=true, to_apply=%region_34.35 | all-reduce | flops 256 | bytes 2048 | tf_op jit(solution)/shard_map/psum | solution.py:90
  905.7 2.6 fusion.136
  910.2 2.4 convolution_bitcast_fusion.25
  922.8 3.4 collective-permute-start.23
  928.0 2.4 maximum_bitcast_fusion.3
  930.5 2.4 convolution_bitcast_fusion.1
  932.8 4.9 collective-permute-done.23
  945.1 38.1 %all-reduce.26 = (f32[128]{0:T(128)S(1)}, f32[128]{0:T(128)S(1)}, f32[3,64,23]{1,2,0:T(8,128)}) all-reduce(f32[128]{0:T(128)S(1)} %get-tuple-element.65, f32[128]{0:T(128)S(1)} %get-tuple-element.64, f32[3,64,23]{1,2,0:T(8,128)S(1)} %fusion.137), channel_id=1, replica_groups=mesh['pix'=8,'ch'=4] {'pix'}, use_global_device_ids=true, to_apply=%region_38.39 | all-reduce | flops 4672 | bytes 37376 | tf_op jit(solution)/shard_map/psum | solution.py:90
  985.0 4.3 convolution_convert_fusion
  1012.7 2.4 maximum_bitcast_fusion
  1015.1 2.5 maximum_bitcast_fusion.2
  1017.6 2.5 maximum_bitcast_fusion.1
  1020.1 11.6 pad_maximum_fusion
  1031.8 20.2 %copy.57 = f32[3,3,3,512,256]{3,2,1,0,4:T(4,128)} copy(f32[3,3,3,512,256]{4,3,2,1,0:T(8,128)} %pad_maximum_fusion) | data formatting | bytes 28311552 | tf_op jit(solution)/shard_map/stack | solution.py:241
  1056.3 2.8 copy.56
  1059.2 4.8 fusion.353
  1064.1 4.5 fusion.367
  1072.2 11.4 psum.158
  1084.2 2.5 multiply_convert_fusion
  1086.7 623.2 %all-reduce.34.cloned.1.call-done = (f32[3,3,128,512]{2,1,0,3:T(4,128)}, f32[3,3,3,512,256]{3,2,1,0,4:T(4,128)}) async-done(((f32[3,3,128,512]{2,1,0,3:T(4,128)}, f32[3,3,3,512,256]{3,2,1,0,4:T(4,128)}), (f32[3,3,128,512]{2,1,0,3:T(4,128)}, f32[3,3,3,512,256]{3,2,1,0,4:T(4,128)})) %all-reduce.34.cloned.1.call-update) | async-done | bytes 16515088
  1715.6 61.0 %reduce-scatter.17.cloned.1.call-done = f32[128,256]{1,0:T(8,128)} async-done(((f32[128,2048]{1,0:T(8,128)}), f32[128,256]{1,0:T(8,128)}) %reduce-scatter.17.cloned.1.call-update) | async-done | bytes 131088 | tf_op jit(solution)/shard_map/reduce_scatter | solution.py:302
  1776.6 66.8 %reduce-scatter.15.cloned.1.call-done = f32[256,128]{1,0:T(8,128)} async-done(((f32[2048,128]{1,0:T(8,128)}), f32[256,128]{1,0:T(8,128)}) %reduce-scatter.15.cloned.1.call-update) | async-done | bytes 131088 | tf_op jit(solution)/shard_map/reduce_scatter | solution.py:300
  (578 shorter events, 185.6 us)
Async XLA Ops:
  7.2 167.5 %copy-start = (bf16[128,2048]{1,0:T(8,128)(2,1)S(1)}, bf16[128,2048]{1,0:T(8,128)(2,1)}, u32[]{:S(2)}) copy-start(bf16[128,2048]{1,0:T(8,128)(2,1)} %param.24) | copy-start | bytes 1572868
  7.2 41.2 %all-gather.5.cloned.1.call-start = ((), (), s32[]{:S(2)}) async-start(), calls=%async_computation.6 | async-start | bytes 5242880 | tf_op jit(solution)/shard_map/all_gather | solution.py:69
  11.0 121.7 %reduce-scatter.19.cloned.1.call-start = ((), (), s32[]{:S(2)}) async-start(), calls=%async_computation.15 | async-start | bytes 1310720
  93.8 6.3 collective-permute-start.1
  95.1 6.4 collective-permute-start
  106.0 67.5 %copy-start.125 = (f32[128]{0:T(128)S(1)}, f32[128]{0:T(128)}, u32[]{:S(2)}) copy-start(f32[128]{0:T(128)} %param.22) | copy-start | bytes 1540
  106.0 68.7 %copy-start.133 = (f32[128]{0:T(128)S(1)}, f32[128]{0:T(128)}, u32[]{:S(2)}) copy-start(f32[128]{0:T(128)} %param.23) | copy-start | bytes 1540
  107.3 113.2 %reduce-scatter.9.cloned.1.call-start = ((), (), s32[]{:S(2)}) async-start(), calls=%async_computation.7 | async-start | bytes 5242880 | tf_op jit(solution)/shard_map/reduce_scatter | solution.py:73
  178.0 160.5 %slice-start = ((s8[7077888]{0:T(1024)(128)(4,1)}), s8[2883584]{0:T(1024)(128)(4,1)S(1)}, s32[]{:S(2)}) async-start(s8[7077888]{0:T(1024)(128)(4,1)} %bitcast.732), calls=%async_computation.17 | async-start | bytes 5767168
  178.0 84.7 %copy-start.104 = (f32[512]{0:T(512)S(1)}, f32[512]{0:T(512)}, u32[]{:S(2)}) copy-start(f32[512]{0:T(512)} %param.25) | copy-start | bytes 6148
  178.1 86.0 %copy-start.108 = (f32[512]{0:T(512)S(1)}, f32[512]{0:T(512)}, u32[]{:S(2)}) copy-start(f32[512]{0:T(512)} %param.26) | copy-start | bytes 6148
  178.1 364.2 %reduce-scatter.11.cloned.1.call-start = ((), (), s32[]{:S(2)}) async-start(), calls=%async_computation.8 | async-start | bytes 1966080 | tf_op jit(solution)/shard_map/reduce_scatter | solution.py:73
  264.0 74.5 %slice-start.1 = ((s8[7077888]{0:T(1024)(128)(4,1)}), s8[4194304]{0:T(1024)(128)(4,1)S(1)}, s32[]{:S(2)}) async-start(s8[7077888]{0:T(1024)(128)(4,1)} %bitcast.732), calls=%async_computation.18 | async-start | bytes 8388608
  266.7 173.8 %copy-start.4 = (bf16[1024,512]{1,0:T(8,128)(2,1)}, bf16[1024,512]{1,0:T(8,128)(2,1)S(1)}, u32[]{:S(2)}) copy-start(bf16[1024,512]{1,0:T(8,128)(2,1)S(1)} %multiply_convert_fusion.1) | copy-start | bytes 3145732
  266.8 67.3 %collective-permute-start.11 = (bf16[8,128,512]{2,1,0:T(8,128)(2,1)S(1)}, bf16[8,128,512]{2,1,0:T(8,128)(2,1)S(1)}, u32[]{:S(2)}, u32[]{:S(2)}) collective-permute-start(bf16[8,128,512]{2,1,0:T(8,128)(2,1)S(1)} %bitcast.736), channel_id=1, source_target_pairs={{20,0},{24,4},{28,8},{21,1},{25,5},{29,9},{22,2},{26,6},{30,10},{2... | collective-permute-start | bytes 3145736 | tf_op jit(solution)/shard_map/ppermute | solution.py:18
  268.1 69.2 %collective-permute-start.10 = (bf16[8,128,512]{2,1,0:T(8,128)(2,1)S(1)}, bf16[8,128,512]{2,1,0:T(8,128)(2,1)S(1)}, u32[]{:S(2)}, u32[]{:S(2)}) collective-permute-start(bf16[8,128,512]{2,1,0:T(8,128)(2,1)S(1)} %bitcast.737), channel_id=1, source_target_pairs={{16,0},{20,4},{24,8},{28,12},{17,1},{21,5},{25,9},{29,13},{18,2},{... | collective-permute-start | bytes 3145736 | tf_op jit(solution)/shard_map/ppermute | solution.py:18
  269.4 69.7 %collective-permute-start.3 = (bf16[8,128,512]{2,1,0:T(8,128)(2,1)S(1)}, bf16[8,128,512]{2,1,0:T(8,128)(2,1)S(1)}, u32[]{:S(2)}, u32[]{:S(2)}) collective-permute-start(bf16[8,128,512]{2,1,0:T(8,128)(2,1)S(1)} %bitcast.738), channel_id=1, source_target_pairs={{0,4},{4,8},{8,12},{12,16},{16,20},{20,24},{24,28},{1,5},{5,9},{9,... | collective-permute-start | bytes 3145736 | tf_op jit(solution)/shard_map/ppermute | solution.py:18
  273.3 90.7 %collective-permute-start.2 = (bf16[8,128,512]{2,1,0:T(8,128)(2,1)S(1)}, bf16[8,128,512]{2,1,0:T(8,128)(2,1)S(1)}, u32[]{:S(2)}, u32[]{:S(2)}) collective-permute-start(bf16[8,128,512]{2,1,0:T(8,128)(2,1)S(1)} %bitcast.739), channel_id=1, source_target_pairs={{0,8},{4,12},{8,16},{12,20},{16,24},{20,28},{1,9},{5,13},{9,17},{1... | collective-permute-start | bytes 3145736 | tf_op jit(solution)/shard_map/ppermute | solution.py:18
  274.7 91.9 %collective-permute-start.5 = (bf16[8,128,512]{2,1,0:T(8,128)(2,1)S(1)}, bf16[8,128,512]{2,1,0:T(8,128)(2,1)S(1)}, u32[]{:S(2)}, u32[]{:S(2)}) collective-permute-start(bf16[8,128,512]{2,1,0:T(8,128)(2,1)S(1)} %bitcast.740), channel_id=1, source_target_pairs={{8,0},{12,4},{16,8},{20,12},{24,16},{28,20},{9,1},{13,5},{17,9},{2... | collective-permute-start | bytes 3145736 | tf_op jit(solution)/shard_map/ppermute | solution.py:18
  334.0 46.5 %collective-permute-start.4 = (bf16[8,128,512]{2,1,0:T(8,128)(2,1)S(1)}, bf16[8,128,512]{2,1,0:T(8,128)(2,1)S(1)}, u32[]{:S(2)}, u32[]{:S(2)}) collective-permute-start(bf16[8,128,512]{2,1,0:T(8,128)(2,1)S(1)} %bitcast.741), channel_id=1, source_target_pairs={{4,0},{8,4},{12,8},{16,12},{20,16},{24,20},{28,24},{5,1},{9,5},{13... | collective-permute-start | bytes 3145736 | tf_op jit(solution)/shard_map/ppermute | solution.py:18
  337.2 100.2 %copy-start.42 = (bf16[8,128,512]{2,1,0:T(8,128)(2,1)}, bf16[8,128,512]{2,1,0:T(8,128)(2,1)S(1)}, u32[]{:S(2)}) copy-start(bf16[8,128,512]{2,1,0:T(8,128)(2,1)S(1)} %get-tuple-element.109) | copy-start | bytes 3145732
  337.2 102.0 %copy-start.38 = (bf16[8,128,512]{2,1,0:T(8,128)(2,1)}, bf16[8,128,512]{2,1,0:T(8,128)(2,1)S(1)}, u32[]{:S(2)}) copy-start(bf16[8,128,512]{2,1,0:T(8,128)(2,1)S(1)} %get-tuple-element.107) | copy-start | bytes 3145732
  337.2 103.8 %copy-start.36 = (bf16[8,128,512]{2,1,0:T(8,128)(2,1)}, bf16[8,128,512]{2,1,0:T(8,128)(2,1)S(1)}, u32[]{:S(2)}) copy-start(bf16[8,128,512]{2,1,0:T(8,128)(2,1)S(1)} %get-tuple-element.106) | copy-start | bytes 3145732
  337.2 105.5 %copy-start.40 = (bf16[8,128,512]{2,1,0:T(8,128)(2,1)}, bf16[8,128,512]{2,1,0:T(8,128)(2,1)S(1)}, u32[]{:S(2)}) copy-start(bf16[8,128,512]{2,1,0:T(8,128)(2,1)S(1)} %get-tuple-element.104) | copy-start | bytes 3145732
  337.2 107.3 %copy-start.32 = (bf16[8,128,512]{2,1,0:T(8,128)(2,1)}, bf16[8,128,512]{2,1,0:T(8,128)(2,1)S(1)}, u32[]{:S(2)}) copy-start(bf16[8,128,512]{2,1,0:T(8,128)(2,1)S(1)} %get-tuple-element.105) | copy-start | bytes 3145732
  337.2 43.8 %collective-permute-start.7 = (bf16[8,128,512]{2,1,0:T(8,128)(2,1)S(1)}, bf16[8,128,512]{2,1,0:T(8,128)(2,1)S(1)}, u32[]{:S(2)}, u32[]{:S(2)}) collective-permute-start(bf16[8,128,512]{2,1,0:T(8,128)(2,1)S(1)} %bitcast.743), channel_id=1, source_target_pairs={{12,0},{16,4},{20,8},{24,12},{28,16},{13,1},{17,5},{21,9},{25,13},... | collective-permute-start | bytes 3145736 | tf_op jit(solution)/shard_map/ppermute | solution.py:18
  339.1 81.2 %collective-permute-start.9 = (bf16[8,128,512]{2,1,0:T(8,128)(2,1)S(1)}, bf16[8,128,512]{2,1,0:T(8,128)(2,1)S(1)}, u32[]{:S(2)}, u32[]{:S(2)}) collective-permute-start(bf16[8,128,512]{2,1,0:T(8,128)(2,1)S(1)} %bitcast.744), channel_id=1, source_target_pairs={{0,16},{4,20},{8,24},{12,28},{1,17},{5,21},{9,25},{13,29},{2,18},{... | collective-permute-start | bytes 3145736 | tf_op jit(solution)/shard_map/ppermute | solution.py:18
  364.1 55.3 %collective-permute-start.6 = (bf16[8,128,512]{2,1,0:T(8,128)(2,1)S(1)}, bf16[8,128,512]{2,1,0:T(8,128)(2,1)S(1)}, u32[]{:S(2)}, u32[]{:S(2)}) collective-permute-start(bf16[8,128,512]{2,1,0:T(8,128)(2,1)S(1)} %bitcast.745), channel_id=1, source_target_pairs={{0,12},{4,16},{8,20},{12,24},{16,28},{1,13},{5,17},{9,21},{13,25},... | collective-permute-start | bytes 3145736 | tf_op jit(solution)/shard_map/ppermute | solution.py:18
  365.6 76.3 %copy-start.10 = (bf16[8,128,512]{2,1,0:T(8,128)(2,1)}, bf16[8,128,512]{2,1,0:T(8,128)(2,1)S(1)}, u32[]{:S(2)}) copy-start(bf16[8,128,512]{2,1,0:T(8,128)(2,1)S(1)} %pad_maximum_fusion.8) | copy-start | bytes 3145732
  365.7 70.7 %copy-start.12 = (bf16[8,128,512]{2,1,0:T(8,128)(2,1)}, bf16[8,128,512]{2,1,0:T(8,128)(2,1)S(1)}, u32[]{:S(2)}) copy-start(bf16[8,128,512]{2,1,0:T(8,128)(2,1)S(1)} %pad_maximum_fusion.5) | copy-start | bytes 3145732
  366.0 56.0 %copy-start.54 = (bf16[8,128,512]{2,1,0:T(8,128)(2,1)}, bf16[8,128,512]{2,1,0:T(8,128)(2,1)S(1)}, u32[]{:S(2)}) copy-start(bf16[8,128,512]{2,1,0:T(8,128)(2,1)S(1)} %get-tuple-element.111) | copy-start | bytes 3145732
  366.0 70.9 %copy-start.58 = (bf16[8,128,512]{2,1,0:T(8,128)(2,1)}, bf16[8,128,512]{2,1,0:T(8,128)(2,1)S(1)}, u32[]{:S(2)}) copy-start(bf16[8,128,512]{2,1,0:T(8,128)(2,1)S(1)} %get-tuple-element.110) | copy-start | bytes 3145732
  366.6 74.8 %copy-start.56 = (bf16[8,128,512]{2,1,0:T(8,128)(2,1)}, bf16[8,128,512]{2,1,0:T(8,128)(2,1)S(1)}, u32[]{:S(2)}) copy-start(bf16[8,128,512]{2,1,0:T(8,128)(2,1)S(1)} %get-tuple-element.117) | copy-start | bytes 3145732
  366.6 75.7 %copy-start.68 = (bf16[8,128,512]{2,1,0:T(8,128)(2,1)}, bf16[8,128,512]{2,1,0:T(8,128)(2,1)S(1)}, u32[]{:S(2)}) copy-start(bf16[8,128,512]{2,1,0:T(8,128)(2,1)S(1)} %get-tuple-element.116) | copy-start | bytes 3145732
  366.6 68.6 %collective-permute-start.8 = (bf16[8,128,512]{2,1,0:T(8,128)(2,1)S(1)}, bf16[8,128,512]{2,1,0:T(8,128)(2,1)S(1)}, u32[]{:S(2)}, u32[]{:S(2)}) collective-permute-start(bf16[8,128,512]{2,1,0:T(8,128)(2,1)S(1)} %bitcast.746), channel_id=1, source_target_pairs={{0,20},{4,24},{8,28},{1,21},{5,25},{9,29},{2,22},{6,26},{10,30},{3... | collective-permute-start | bytes 3145736 | tf_op jit(solution)/shard_map/ppermute | solution.py:18
  380.7 62.9 %copy-start.8 = (bf16[8,128,512]{2,1,0:T(8,128)(2,1)}, bf16[8,128,512]{2,1,0:T(8,128)(2,1)S(1)}, u32[]{:S(2)}) copy-start(bf16[8,128,512]{2,1,0:T(8,128)(2,1)S(1)} %pad_maximum_fusion.6) | copy-start | bytes 3145732
  381.0 62.2 %copy-start.48 = (bf16[8,128,512]{2,1,0:T(8,128)(2,1)}, bf16[8,128,512]{2,1,0:T(8,128)(2,1)S(1)}, u32[]{:S(2)}) copy-start(bf16[8,128,512]{2,1,0:T(8,128)(2,1)S(1)} %get-tuple-element.103) | copy-start | bytes 3145732
  381.0 63.1 %copy-start.64 = (bf16[8,128,512]{2,1,0:T(8,128)(2,1)}, bf16[8,128,512]{2,1,0:T(8,128)(2,1)S(1)}, u32[]{:S(2)}) copy-start(bf16[8,128,512]{2,1,0:T(8,128)(2,1)S(1)} %get-tuple-element.102) | copy-start | bytes 3145732
  447.4 228.0 %all-gather.7.cloned.1.call-start = ((), (), s32[]{:S(2)}) async-start(), calls=%async_computation.9 | async-start | bytes 1966080 | tf_op jit(solution)/shard_map/all_gather | solution.py:69
  449.9 84.9 %copy-start.123 = (f32[3,64]{1,0:T(4,128)S(1)}, f32[3,64]{1,0:T(4,128)}, u32[]{:S(2)}) copy-start(f32[3,64]{1,0:T(4,128)} %param.28) | copy-start | bytes 2308
  449.9 85.0 %copy-start.124 = (f32[3,64]{1,0:T(4,128)S(1)}, f32[3,64]{1,0:T(4,128)}, u32[]{:S(2)}) copy-start(f32[3,64]{1,0:T(4,128)} %param.29) | copy-start | bytes 2308
  542.2 73.6 %copy-start.72 = (f32[1,3,1024,64]{2,0,3,1:T(1,128)S(1)}, f32[1,3,1024,64]{2,0,3,1:T(1,128)}, u32[]{:S(2)}) copy-start(f32[1,3,1024,64]{2,0,3,1:T(1,128)} %fusion) | copy-start | bytes 2359300
  544.0 74.7 %copy-start.6 = (f32[3,1024,64]{1,0,2:T(4,128)}, f32[3,1024,64]{1,0,2:T(4,128)S(1)}, u32[]{:S(2)}) copy-start(f32[3,1024,64]{1,0,2:T(4,128)S(1)} %reshape.408) | copy-start | bytes 2359300
  657.8 222.2 %all-gather.9.cloned.1.call-start = ((), (), s32[]{:S(2)}) async-start(), calls=%async_computation.10 | async-start | bytes 5242880 | tf_op jit(solution)/shard_map/all_gather | solution.py:69
  677.0 26.9 %collective-permute-start.21 = (bf16[8,128,256]{1,0,2:T(8,128)(2,1)S(1)}, bf16[8,128,256]{1,0,2:T(8,128)(2,1)S(1)}, u32[]{:S(2)}, u32[]{:S(2)}) collective-permute-start(bf16[8,128,256]{1,0,2:T(8,128)(2,1)S(1)} %bitcast.843), channel_id=1, source_target_pairs={{0,16},{4,20},{8,24},{12,28},{1,17},{5,21},{9,25},{13,29},{2,18},{... | collective-permute-start | bytes 1572872 | tf_op jit(solution)/shard_map/ppermute | solution.py:18
  681.6 23.6 %collective-permute-start.20 = (bf16[8,128,256]{1,0,2:T(8,128)(2,1)S(1)}, bf16[8,128,256]{1,0,2:T(8,128)(2,1)S(1)}, u32[]{:S(2)}, u32[]{:S(2)}) collective-permute-start(bf16[8,128,256]{1,0,2:T(8,128)(2,1)S(1)} %bitcast.844), channel_id=1, source_target_pairs={{0,20},{4,24},{8,28},{1,21},{5,25},{9,29},{2,22},{6,26},{10,30},{3... | collective-permute-start | bytes 1572872 | tf_op jit(solution)/shard_map/ppermute | solution.py:18
  683.8 41.1 %collective-permute-start.19 = (bf16[8,128,256]{1,0,2:T(8,128)(2,1)S(1)}, bf16[8,128,256]{1,0,2:T(8,128)(2,1)S(1)}, u32[]{:S(2)}, u32[]{:S(2)}) collective-permute-start(bf16[8,128,256]{1,0,2:T(8,128)(2,1)S(1)} %bitcast.845), channel_id=1, source_target_pairs={{20,0},{24,4},{28,8},{21,1},{25,5},{29,9},{22,2},{26,6},{30,10},{2... | collective-permute-start | bytes 1572872 | tf_op jit(solution)/shard_map/ppermute | solution.py:18
  685.1 50.8 %collective-permute-start.18 = (bf16[8,128,256]{1,0,2:T(8,128)(2,1)S(1)}, bf16[8,128,256]{1,0,2:T(8,128)(2,1)S(1)}, u32[]{:S(2)}, u32[]{:S(2)}) collective-permute-start(bf16[8,128,256]{1,0,2:T(8,128)(2,1)S(1)} %bitcast.846), channel_id=1, source_target_pairs={{16,0},{20,4},{24,8},{28,12},{17,1},{21,5},{25,9},{29,13},{18,2},{... | collective-permute-start | bytes 1572872 | tf_op jit(solution)/shard_map/ppermute | solution.py:18
  686.9 52.7 %collective-permute-start.15 = (bf16[8,128,256]{1,0,2:T(8,128)(2,1)S(1)}, bf16[8,128,256]{1,0,2:T(8,128)(2,1)S(1)}, u32[]{:S(2)}, u32[]{:S(2)}) collective-permute-start(bf16[8,128,256]{1,0,2:T(8,128)(2,1)S(1)} %bitcast.838), channel_id=1, source_target_pairs={{0,4},{4,8},{8,12},{12,16},{16,20},{20,24},{24,28},{1,5},{5,9},{9,... | collective-permute-start | bytes 1572872 | tf_op jit(solution)/shard_map/ppermute | solution.py:18
  703.9 37.3 %collective-permute-start.13 = (bf16[8,128,256]{1,0,2:T(8,128)(2,1)S(1)}, bf16[8,128,256]{1,0,2:T(8,128)(2,1)S(1)}, u32[]{:S(2)}, u32[]{:S(2)}) collective-permute-start(bf16[8,128,256]{1,0,2:T(8,128)(2,1)S(1)} %bitcast.840), channel_id=1, source_target_pairs={{8,0},{12,4},{16,8},{20,12},{24,16},{28,20},{9,1},{13,5},{17,9},{2... | collective-permute-start | bytes 1572872 | tf_op jit(solution)/shard_map/ppermute | solution.py:18
  705.2 36.0 %collective-permute-start.12 = (bf16[8,128,256]{1,0,2:T(8,128)(2,1)S(1)}, bf16[8,128,256]{1,0,2:T(8,128)(2,1)S(1)}, u32[]{:S(2)}, u32[]{:S(2)}) collective-permute-start(bf16[8,128,256]{1,0,2:T(8,128)(2,1)S(1)} %bitcast.841), channel_id=1, source_target_pairs={{4,0},{8,4},{12,8},{16,12},{20,16},{24,20},{28,24},{5,1},{9,5},{13... | collective-permute-start | bytes 1572872 | tf_op jit(solution)/shard_map/ppermute | solution.py:18
  724.9 21.3 %collective-permute-start.14 = (bf16[8,128,256]{1,0,2:T(8,128)(2,1)S(1)}, bf16[8,128,256]{1,0,2:T(8,128)(2,1)S(1)}, u32[]{:S(2)}, u32[]{:S(2)}) collective-permute-start(bf16[8,128,256]{1,0,2:T(8,128)(2,1)S(1)} %bitcast.842), channel_id=1, source_target_pairs={{0,8},{4,12},{8,16},{12,20},{16,24},{20,28},{1,9},{5,13},{9,17},{1... | collective-permute-start | bytes 1572872 | tf_op jit(solution)/shard_map/ppermute | solution.py:18
  735.9 31.2 %collective-permute-start.17 = (bf16[8,128,256]{1,0,2:T(8,128)(2,1)S(1)}, bf16[8,128,256]{1,0,2:T(8,128)(2,1)S(1)}, u32[]{:S(2)}, u32[]{:S(2)}) collective-permute-start(bf16[8,128,256]{1,0,2:T(8,128)(2,1)S(1)} %bitcast.836), channel_id=1, source_target_pairs={{0,12},{4,16},{8,20},{12,24},{16,28},{1,13},{5,17},{9,21},{13,25},... | collective-permute-start | bytes 1572872 | tf_op jit(solution)/shard_map/ppermute | solution.py:18
  739.6 31.6 %collective-permute-start.16 = (bf16[8,128,256]{1,0,2:T(8,128)(2,1)S(1)}, bf16[8,128,256]{1,0,2:T(8,128)(2,1)S(1)}, u32[]{:S(2)}, u32[]{:S(2)}) collective-permute-start(bf16[8,128,256]{1,0,2:T(8,128)(2,1)S(1)} %bitcast.837), channel_id=1, source_target_pairs={{12,0},{16,4},{20,8},{24,12},{28,16},{13,1},{17,5},{21,9},{25,13},... | collective-permute-start | bytes 1572872 | tf_op jit(solution)/shard_map/ppermute | solution.py:18
  849.0 72.7 %all-gather.11.cloned.1.call-start = ((), (), s32[]{:S(2)}) async-start(), calls=%async_computation.11 | async-start | bytes 1310720 | tf_op jit(solution)/shard_map/all_gather | solution.py:69
  852.7 53.0 %copy-start.117 = (f32[128]{0:T(128)S(1)}, f32[128]{0:T(128)}, u32[]{:S(2)}) copy-start(f32[128]{0:T(128)} %get-tuple-element.83) | copy-start | bytes 1540
  852.8 55.7 %copy-start.13 = (bf16[8,128,512]{2,1,0:T(8,128)(2,1)S(1)}, bf16[8,128,512]{2,1,0:T(8,128)(2,1)}, u32[]{:S(2)}) copy-start(bf16[8,128,512]{2,1,0:T(8,128)(2,1)} %copy-done.12) | copy-start | bytes 3145732
  908.4 175.9 %reduce-scatter.13.cloned.1.call-start = ((), (), s32[]{:S(2)}) async-start(), calls=%async_computation.12 | async-start | bytes 5242880 | tf_op jit(solution)/shard_map/reduce_scatter | solution.py:73
  922.8 15.0 collective-permute-start.23
  926.2 11.6 collective-permute-start.22
  989.4 720.6 %all-reduce.34.cloned.1.call-start = ((), (), s32[]{:S(2)}) async-start(), calls=%async_computation.16 | async-start | bytes 44040192
  1059.2 717.5 %reduce-scatter.17.cloned.1.call-start = ((), (), s32[]{:S(2)}) async-start(), calls=%async_computation.14 | async-start | bytes 1179648 | tf_op jit(solution)/shard_map/reduce_scatter | solution.py:302
  1064.1 779.4 %reduce-scatter.15.cloned.1.call-start = ((), (), s32[]{:S(2)}) async-start(), calls=%async_computation.13 | async-start | bytes 1179648 | tf_op jit(solution)/shard_map/reduce_scatter | solution.py:300
  1711.7 131.7 %copy-start.1 = (bf16[128,2048]{1,0:T(8,128)(2,1)S(1)}, bf16[128,2048]{1,0:T(8,128)(2,1)}, u32[]{:S(2)}) copy-start(bf16[128,2048]{1,0:T(8,128)(2,1)} %param.24) | copy-start | bytes 1572868
  (115 other events, 1129.8 us)
Sparse Core Ops, SparseCore 0:
  11.2 37.1 all-gather.4
  107.5 25.2 reduce-scatter.18
  178.2 42.2 reduce-scatter.8
  447.5 48.6 reduce-scatter.10
  657.9 17.4 all-gather.6
  849.1 30.7 all-gather.8
  908.5 13.1 all-gather.10
  989.5 40.8 reduce-scatter.12
  1059.3 650.6 all-reduce.33
  1713.8 62.8 reduce-scatter.16
  1781.0 62.4 reduce-scatter.14
where the time goes:
time: 1860 us; the launch traced here: 1850 us
  waiting for transfers between devices  1060 us (57%)
  blocking collectives  375 us (20%)
  matrix products  164 us (9%)
  starting transfers between devices  93.6 us (5%)
  local copies, waits for them, and re-layouts  70 us (4%)
  other arithmetic  66.4 us (4%)
  between operations  26.1 us (1%)
    unnamed x13, waiting for transfers between devices  649 us
    ppermute x20, waiting for transfers between devices, from_behind(): lax.ppermute(value, axis, [(source, source + steps) for source in range(f...  147 us
    psum x4, blocking collectives, norm_grad(): lax.psum((jnp.sum(grad_out, axis=axes, keepdims=True), jnp.sum(grad_out *...  118 us
    psum x4, blocking collectives, normalized(): lax.psum((jnp.sum(hidden * valid, axis=axes, keepdims=True), jnp.sum(vali...  101 us
    psum x4, blocking collectives, normalized(): lax.psum(jnp.sum(valid * (hidden - center) ** 2, axis=axes, keepdims=True...  84.5 us
    all_gather x4, waiting for transfers between devices, gather_channels(): return lax.all_gather(value, 'ch', axis=1, tiled=True)  82.8 us
    ppermute x20, starting transfers between devices, from_behind(): lax.ppermute(value, axis, [(source, source + steps) for source in range(f...  81.8 us
    dot_general x27, matrix products, on_device(): jnp.einsum('pa,ca->pc', shifted.reshape(pixels, -1), aspp_weight[j, a, b]...  69 us
  transfers between devices with their start and end apart: 35, of which 17 were waited for; matrix products, arithmetic and copies ran while one was open for 8% of the time, Pallas kernels for 0%

commit v1 on v0

--- a/solution.py
+++ b/solution.py
@@ -1,6 +1,8 @@
 import jax
 import jax.numpy as jnp
 from jax import lax
+from jax.experimental import pallas as pl
+from jax.experimental.pallas import tpu as pltpu
 from jax.sharding import PartitionSpec as P
 
 CLS = 19
@@ -321,6 +323,1378 @@
     )
 
 
+MESH = pl.DeviceIdType.MESH
+ROW_CLASSES, COL_CLASSES = 2, 4
+PHASES = ROW_CLASSES * COL_CLASSES
+SPLIT = 4
+FAR_FIRST = (6, 7, 4, 5, 2, 3, 1)
+f32, bf16 = jnp.float32, jnp.bfloat16
+VMEM_BYTES = 60 << 20
+
+
+def shape(dims, dtype):
+    return jax.ShapeDtypeStruct(dims, dtype)
+
+
+def call(name, cid, kernel, arrays, outs, scratch):
+    vmem = pl.BlockSpec(memory_space=pltpu.VMEM)
+    return pl.pallas_call(
+        kernel,
+        out_shape=outs,
+        in_specs=[vmem] * len(arrays),
+        out_specs=[vmem] * len(outs),
+        scratch_shapes=scratch,
+        compiler_params=pltpu.CompilerParams(
+            collective_id=cid, has_side_effects=True, vmem_limit_bytes=VMEM_BYTES
+        ),
+        name=name,
+    )(*arrays)
+
+
+def dma(*dims):
+    return pltpu.SemaphoreType.DMA(dims)
+
+
+def greet(ch, pix):
+    p, c = lax.axis_index("pix"), lax.axis_index("ch")
+    barrier = pltpu.get_barrier_semaphore()
+    for k in ch:
+        pl.semaphore_signal(barrier, inc=1, device_id=(p, c ^ k), device_id_type=MESH)
+    for k in pix:
+        pl.semaphore_signal(barrier, inc=1, device_id=(p ^ k, c), device_id_type=MESH)
+    return barrier, len(ch) + len(pix)
+
+
+def push(src, dst, send, recv, device):
+    copy = pltpu.make_async_remote_copy(
+        src_ref=src,
+        dst_ref=dst,
+        send_sem=send,
+        recv_sem=recv,
+        device_id=device,
+        device_id_type=MESH,
+    )
+    copy.start()
+    return copy
+
+
+def keep(src, dst, sem):
+    copy = pltpu.make_async_copy(src, dst, sem)
+    copy.start()
+    return copy
+
+
+def rows(start, size):
+    return pl.ds(pl.multiple_of(start, size), size)
+
+
+def fold(x):
+    return jnp.sum(x.reshape(x.shape[0] // 8, 8, x.shape[1]), axis=0)
+
+
+def total(x):
+    return jnp.sum(x, axis=0, keepdims=True)
+
+
+def loop(steps, body, init):
+    return lax.fori_loop(0, steps, body, init)
+
+
+def sum_over_ch(part, tile, tiles, own, out, near, cross, near_sems, far_sems):
+    p, c = lax.axis_index("pix"), lax.axis_index("ch")
+    k, x = lax.rem(c, 2), c // 2
+    n = own.shape[2]
+    copies = []
+    for t in range(tiles):
+        at = pl.ds(t * tile, tile)
+        value = part(t)
+        for d in range(SPLIT):
+            block = value[:, d * n : (d + 1) * n]
+            own[d, at] = block
+            out[d, at] = block.astype(bf16)
+        copies.append(
+            [
+                push(
+                    out.at[2 * h + 1 - k, at],
+                    near.at[h, at],
+                    near_sems.at[0, t, h],
+                    near_sems.at[1, t, h],
+                    (p, c ^ 1),
+                )
+                for h in range(2)
+            ]
+        )
+    crossing = []
+    for t in range(tiles):
+        at = pl.ds(t * tile, tile)
+        for copy in copies[t]:
+            copy.wait()
+        cross[0, at] = (own[2 * (1 - x) + k, at] + near[1 - x, at].astype(f32)).astype(bf16)
+        crossing.append(
+            push(cross.at[0, at], cross.at[1, at], far_sems.at[0, t], far_sems.at[1, t], (p, c ^ 2))
+        )
+
+    def result(t):
+        at = pl.ds(t * tile, tile)
+        crossing[t].wait()
+        return own[2 * x + k, at] + near[x, at].astype(f32) + cross[1, at].astype(f32)
+
+    return result
+
+
+def sum_scratch(pixels, n, tiles):
+    return [
+        pltpu.VMEM((SPLIT, pixels, n), f32),
+        pltpu.VMEM((SPLIT, pixels, n), bf16),
+        pltpu.VMEM((2, pixels, n), bf16),
+        pltpu.VMEM((2, pixels, n), bf16),
+        dma(2, tiles, 2),
+        dma(2, tiles),
+    ]
+
+
+def pix_exchange(send, recv, sems):
+    p, c = lax.axis_index("pix"), lax.axis_index("ch")
+    copies = [
+        push(send, recv.at[p], sems.at[0, k], sems.at[1, k], (p ^ k, c)) for k in FAR_FIRST
+    ]
+    recv[p] = send[...]
+    for copy in copies:
+        copy.wait()
+
+
+def norm_stats(hidden, valid, pixels, send, recv, sems):
+    n = hidden.shape[1]
+    tile = 128
+    repeat = n // 128
+
+    def mask(at):
+        v = valid[at]
+        return v if repeat == 1 else jnp.concatenate([v] * repeat, axis=1)
+
+    def first(i, carry):
+        at = rows(i * tile, tile)
+        v = mask(at)
+        return carry[0] + fold(hidden[at] * v), carry[1] + fold(v)
+
+    zero = jnp.zeros((8, n), f32)
+    sums, count = loop(pixels // tile, first, (zero, zero))
+    sums, count = total(sums), total(count)
+    center = sums / jnp.maximum(count, 1.0)
+
+    def second(i, carry):
+        at = rows(i * tile, tile)
+        apart = hidden[at] - center
+        return carry + fold(mask(at) * apart * apart)
+
+    spread = total(loop(pixels // tile, second, zero))
+    send[0:1] = sums
+    send[1:2] = spread
+    send[2:3] = count
+    pix_exchange(send, recv, sems)
+    return join(recv, PHASES)
+
+
+def join(recv, parts):
+    sums, count = recv[0, 0:1], recv[0, 2:3]
+    for i in range(1, parts):
+        sums, count = sums + recv[i, 0:1], count + recv[i, 2:3]
+    center = sums / count
+    spread = jnp.zeros_like(sums)
+    for i in range(parts):
+        n = recv[i, 2:3]
+        apart = recv[i, 0:1] / jnp.maximum(n, 1.0) - center
+        spread = spread + recv[i, 1:2] + n * apart * apart
+    return center, lax.rsqrt(spread / count + epsilon), count
+
+
+def stat_scratch(n):
+    return [pltpu.VMEM((8, n), f32), pltpu.VMEM((PHASES, 8, n), f32), dma(2, PHASES)]
+
+
+def silu(x):
+    return x / (1.0 + jnp.exp(-x))
+
+
+def gather_over_ch(full, n, tile, tiles, near_sems, far_sems, hop_sems, ready):
+    p, c = lax.axis_index("pix"), lax.axis_index("ch")
+
+    def part(owner, t):
+        return full.at[pl.ds(t * tile, tile), rows(owner * n, n)]
+
+    near, far, hops = [], [], []
+    for t in range(tiles):
+        ready(t)
+        src = part(c, t)
+        far.append(push(src, src, far_sems.at[0, t], far_sems.at[1, t], (p, c ^ 2)))
+        near.append(push(src, src, near_sems.at[0, t], near_sems.at[1, t], (p, c ^ 1)))
+    for t in range(tiles):
+        far[t].wait_recv()
+        src = part(c ^ 2, t)
+        hops.append(push(src, src, hop_sems.at[0, t], hop_sems.at[1, t], (p, c ^ 1)))
+    for t in range(tiles):
+        far[t].wait_send()
+        near[t].wait()
+        hops[t].wait()
+
+
+def gather_scratch(tiles):
+    return [dma(2, tiles), dma(2, tiles), dma(2, tiles)]
+
+
+def to_classes(x):
+    rows, cols, n = x.shape
+    x = x.reshape(rows // ROW_CLASSES, ROW_CLASSES, cols // COL_CLASSES, COL_CLASSES, n)
+    return x.transpose(1, 3, 0, 2, 4).reshape(PHASES, -1, n)
+
+
+def from_classes(x, rows, cols):
+    n = x.shape[-1]
+    x = x.reshape(ROW_CLASSES, COL_CLASSES, rows // ROW_CLASSES, cols // COL_CLASSES, n)
+    return x.transpose(2, 0, 3, 1, 4).reshape(rows, cols, n)
+
+
+TILES = 4
+
+
+def stage_one(feat, valid, weight, expand, affine, heads, targets, square, *refs):
+    (masked, reduce_rows, expand_cols, heads_all, targets_all, square_all, norm, padded, stat) = refs[:9]
+    (wide, hidden, own, out, near, cross, near_sems, far_sems, send, recv, stat_sems) = refs[9:20]
+    (weight_sems, pix_sems, local_sems, halo_sems) = refs[20:]
+    p, c = lax.axis_index("pix"), lax.axis_index("ch")
+    pixels, local_in = feat.shape
+    local_mid = weight.shape[1]
+    tile = pixels // TILES
+    barrier, expected = greet((1, 2, 3), FAR_FIRST)
+    for r in range(8):
+        for g in range(local_in // 128):
+            lanes = slice(g * 128, (g + 1) * 128)
+            wide[g] = feat[r * 128 : (r + 1) * 128, lanes].astype(f32)
+            for b in range(COL_CLASSES):
+                block = ((r % ROW_CLASSES) * COL_CLASSES + b) * 128 + (r // ROW_CLASSES) * 32
+                value = wide[g, pl.ds(b, 32, stride=COL_CLASSES), :] * valid[block : block + 32]
+                masked[block : block + 32, lanes] = value.astype(bf16)
+    pl.semaphore_wait(barrier, expected)
+
+    def pieces(to):
+        return (
+            (weight.at[rows(to * local_in, local_in), :], reduce_rows.at[:, rows(c * local_mid, local_mid)]),
+            (expand.at[:, rows(to * local_in, local_in)], expand_cols.at[rows(c * local_mid, local_mid), :]),
+            (heads, heads_all.at[c]),
+        )
+
+    copies = [
+        [push(*pieces(c ^ k)[i], weight_sems.at[0, k, i], weight_sems.at[1, k, i], (p, c ^ k)) for k in (2, 3, 1)]
+        for i in range(3)
+    ]
+    local = [keep(*pieces(c)[i], local_sems.at[i]) for i in range(3)]
+    local.append(keep(targets.at[p], targets_all.at[p], local_sems.at[3]))
+    local.append(keep(square, square_all.at[p], local_sems.at[4]))
+    routed = [
+        push(targets.at[p ^ k], targets_all.at[p], pix_sems.at[0, k, 0], pix_sems.at[1, k, 0], (p ^ k, c))
+        for k in FAR_FIRST
+    ] + [push(square, square_all.at[p], pix_sems.at[0, k, 1], pix_sems.at[1, k, 1], (p ^ k, c)) for k in FAR_FIRST]
+    for copy in copies[0]:
+        copy.wait()
+    local[0].wait()
+
+    def part(t):
+        return jnp.dot(masked[t * tile : (t + 1) * tile], reduce_rows[...], preferred_element_type=f32)
+
+    result = sum_over_ch(part, tile, TILES, own, out, near, cross, near_sems, far_sems)
+    for t in range(TILES):
+        hidden[t * tile : (t + 1) * tile] = result(t)
+    for copy in routed + copies[1] + copies[2] + local[1:]:
+        copy.wait()
+    center, scale, count = norm_stats(hidden, valid, pixels, send, recv, stat_sems)
+    stat[0:1] = center
+    stat[1:2] = scale
+    stat[2:3] = count
+    for i in range(PHASES):
+        at = pl.ds(i * 128, 128)
+        value = (hidden[at] - center) * scale
+        norm[at] = value
+        act = silu(value * affine[0:1] + affine[1:2]) * valid[at]
+        padded[i, 1:5] = act.astype(bf16).reshape(4, 32, local_mid)
+    up = lambda: pltpu.make_async_remote_copy(
+        src_ref=padded.at[:, 4],
+        dst_ref=padded.at[:, 0],
+        send_sem=halo_sems.at[0, 0],
+        recv_sem=halo_sems.at[1, 0],
+        device_id=(p + 1, c),
+        device_id_type=MESH,
+    )
+    down = lambda: pltpu.make_async_remote_copy(
+        src_ref=padded.at[:, 1],
+        dst_ref=padded.at[:, 5],
+        send_sem=halo_sems.at[0, 1],
+        recv_sem=halo_sems.at[1, 1],
+        device_id=(p - 1, c),
+        device_id_type=MESH,
+    )
+    first, last = p == 0, p == PHASES - 1
+
+    @pl.when(jnp.logical_not(last))
+    def _():
+        up().start()
+
+    @pl.when(jnp.logical_not(first))
+    def _():
+        down().start()
+
+    @pl.when(last)
+    def _():
+        padded[:, 5] = jnp.zeros((PHASES, 32, local_mid), bf16)
+
+    @pl.when(first)
+    def _():
+        padded[:, 0] = jnp.zeros((PHASES, 32, local_mid), bf16)
+
+    @pl.when(jnp.logical_not(last))
+    def _():
+        up().wait_send()
+        down().wait_recv()
+
+    @pl.when(jnp.logical_not(first))
+    def _():
+        down().wait_send()
+        up().wait_recv()
+
+
+def run_stage_one(cid, feat, valid, weight, expand, affine, heads, targets, square):
+    pixels, local_in = feat.shape
+    local_mid = weight.shape[1]
+    mid = SPLIT * local_mid
+    outs = [
+        shape((pixels, local_in), bf16),
+        shape((local_in, mid), bf16),
+        shape((mid, local_in), bf16),
+        shape((SPLIT,) + heads.shape, f32),
+        shape(targets.shape, f32),
+        shape((PHASES,) + square.shape, f32),
+        shape((pixels, local_mid), f32),
+        shape((PHASES, 6, 32, local_mid), bf16),
+        shape((8, local_mid), f32),
+    ]
+    scratch = (
+        [pltpu.VMEM((local_in // 128, 128, 128), f32), pltpu.VMEM((pixels, local_mid), f32)]
+        + sum_scratch(pixels, local_mid, TILES)
+        + stat_scratch(local_mid)
+        + [dma(2, SPLIT, 3), dma(2, PHASES, 2), dma(5), dma(2, 2)]
+    )
+    return call("stage_one", cid, stage_one, [feat, valid, weight, expand, affine, heads, targets, square], outs, scratch)
+
+
+def stage_two(padded, valid, weight, affine, *refs):
+    (norm, full, taps, stat) = refs[:4]
+    (hidden, own, out, near, cross, near_sems, far_sems, send, recv, stat_sems) = refs[4:14]
+    (g_near, g_far, g_hop) = refs[14:]
+    p, c = lax.axis_index("pix"), lax.axis_index("ch")
+    pixels = valid.shape[0]
+    local_mid = padded.shape[3]
+    tile = pixels // TILES
+    barrier, expected = greet((1, 2), FAR_FIRST)
+    place = lax.broadcasted_iota(jnp.int32, (192, local_mid), 0) % 32
+    for i in range(PHASES):
+        beta = i % COL_CLASSES
+        plain = padded[i].reshape(192, local_mid)
+        wide = plain.astype(f32)
+        if beta >= 2:
+            moved_by = jnp.where(place == 0, 0.0, pltpu.roll(wide, 1, 0)).astype(bf16)
+        else:
+            moved_by = jnp.where(place == 31, 0.0, pltpu.roll(wide, 191, 0)).astype(bf16)
+        for a in range(3):
+            at = slice(a * 32, a * 32 + 128)
+            for b, other, value in (
+                (1, beta, plain),
+                (0, (beta + 2) % 4, moved_by if beta >= 2 else plain),
+                (2, (beta + 2) % 4, plain if beta >= 2 else moved_by),
+            ):
+                to = (i - beta + other) * 128
+                col = (a * 3 + b) * local_mid
+                taps[to : to + 128, col : col + local_mid] = value[at]
+    pl.semaphore_wait(barrier, expected)
+
+    def part(t):
+        return jnp.dot(taps[t * tile : (t + 1) * tile], weight[...], preferred_element_type=f32)
+
+    result = sum_over_ch(part, tile, TILES, own, out, near, cross, near_sems, far_sems)
+    for t in range(TILES):
+        hidden[t * tile : (t + 1) * tile] = result(t)
+    center, scale, count = norm_stats(hidden, valid, pixels, send, recv, stat_sems)
+    stat[0:1] = center
+    stat[1:2] = scale
+    stat[2:3] = count
+
+    def ready(t):
+        for i in range(tile // 128):
+            at = pl.ds(t * tile + i * 128, 128)
+            value = (hidden[at] - center) * scale
+            norm[at] = value
+            act = silu(value * affine[0:1] + affine[1:2]) * valid[at]
+            full[at, rows(c * local_mid, local_mid)] = act.astype(bf16)
+
+    gather_over_ch(full, local_mid, tile, TILES, g_near, g_far, g_hop, ready)
+
+
+def run_stage_two(cid, padded, valid, weight, affine):
+    pixels, local_mid = valid.shape[0], padded.shape[3]
+    outs = [
+        shape((pixels, local_mid), f32),
+        shape((pixels, SPLIT * local_mid), bf16),
+        shape((pixels, 9 * local_mid), bf16),
+        shape((8, local_mid), f32),
+    ]
+    scratch = (
+        [pltpu.VMEM((pixels, local_mid), f32)]
+        + sum_scratch(pixels, local_mid, TILES)
+        + stat_scratch(local_mid)
+        + gather_scratch(TILES)
+    )
+    return call("stage_two", cid, stage_two, [padded, valid, weight, affine], outs, scratch)
+
+
+def stage_three(full, weight, masked, valid, affine, *refs):
+    (norm, classes, stat) = refs[:3]
+    (hidden, trunk, send, recv, stat_sems, class_sems, own_sem) = refs[3:]
+    p, c = lax.axis_index("pix"), lax.axis_index("ch")
+    pixels, n = masked.shape
+    barrier, expected = greet((), FAR_FIRST)
+    tile = pixels // TILES
+    for t in range(TILES):
+        at = pl.ds(t * tile, tile)
+        hidden[at] = jnp.dot(full[at], weight[...], preferred_element_type=f32)
+    pl.semaphore_wait(barrier, expected)
+    center, scale, count = norm_stats(hidden, valid, pixels, send, recv, stat_sems)
+    stat[0:1] = center
+    stat[1:2] = scale
+    stat[2:3] = count
+
+    def finish(to):
+        def half(i, carry):
+            at = rows(to * 128 + i * 32, 32)
+            value = (hidden[at] - center) * scale
+            norm[at] = value
+            pre = value * affine[0:1] + affine[1:2] + masked[at].astype(f32)
+            v = valid[at]
+            trunk[at] = (silu(pre) * jnp.concatenate([v] * (n // 128), axis=1)).astype(bf16)
+            return carry
+
+        loop(4, half, 0)
+
+    copies = []
+    for k in FAR_FIRST:
+        to = p ^ k
+        finish(to)
+        copies.append(
+            push(
+                trunk.at[rows(to * 128, 128)],
+                classes.at[rows(p * 128, 128)],
+                class_sems.at[0, k],
+                class_sems.at[1, k],
+                (to, c),
+            )
+        )
+    finish(p)
+    copies.append(keep(trunk.at[rows(p * 128, 128)], classes.at[rows(p * 128, 128)], own_sem.at[0]))
+    for copy in copies:
+        copy.wait()
+
+
+def run_stage_three(cid, full, weight, masked, valid, affine):
+    pixels, n = masked.shape
+    outs = [shape((pixels, n), f32), shape((pixels, n), bf16), shape((8, n), f32)]
+    scratch = (
+        [pltpu.VMEM((pixels, n), f32), pltpu.VMEM((pixels, n), bf16)]
+        + stat_scratch(n)
+        + [dma(2, PHASES), dma(1)]
+    )
+    return call("stage_three", cid, stage_three, [full, weight, masked, valid, affine], outs, scratch)
+
+
+RATE_ROWS = tuple(rate // ROW_CLASSES for rate in aspp_rates)
+RATE_COLS = tuple(rate // COL_CLASSES for rate in aspp_rates)
+
+
+def load_pyramid(weight, wide, sems):
+    m = weight.shape[4]
+    return [
+        [keep(weight.at[j, a, b], wide.at[3 * j + a, :, b * m : (b + 1) * m], sems.at[3 * j + a, b]) for b in range(3)]
+        for j in range(3)
+        for a in range(3)
+    ]
+
+
+def move_cols(x, by):
+    place = lax.broadcasted_iota(jnp.int32, x.shape, 0) % 32
+    rolled = pltpu.roll(x, by % x.shape[0], 0)
+    return jnp.where(place < by, 0.0, rolled) if by > 0 else jnp.where(place >= 32 + by, 0.0, rolled)
+
+
+def ch_exchange(send, recv, sems):
+    p, c = lax.axis_index("pix"), lax.axis_index("ch")
+    copies = [push(send, recv.at[c], sems.at[0, k], sems.at[1, k], (p, c ^ k)) for k in (2, 3, 1)]
+    recv[c] = send[...]
+    for copy in copies:
+        copy.wait()
+
+
+def add_up(recv, parts):
+    value = recv[0]
+    for i in range(1, parts):
+        value = value + recv[i]
+    return value
+
+
+def task_vector(square, weights):
+    product = square * weights
+    row = lax.broadcasted_iota(jnp.int32, (32, 32), 0)
+    col = lax.broadcasted_iota(jnp.int32, (32, 32), 1)
+
+    def task(i):
+        return (i >= CLS).astype(jnp.int32) + (i >= CLS + 1).astype(jnp.int32)
+
+    def entry(t, s):
+        return jnp.sum(
+            jnp.sum(jnp.where((task(row) == t) & (task(col) == s), product, 0.0), axis=1, keepdims=True),
+            axis=0,
+            keepdims=True,
+        )
+
+    gram = [[entry(t, s) for s in range(3)] for t in range(3)]
+    norms = [jnp.sqrt(gram[k][k] + 1e-06) for k in range(3)]
+    proj = [[gram[i][k] / norms[k] for k in range(3)] for i in range(3)]
+    vector = [proj[0][0] - proj[0][b] for b in (1, 2)]
+    matrix = [[proj[0][0] - proj[0][b] - proj[a][0] + proj[a][b] for b in (1, 2)] for a in (1, 2)]
+    determinant = matrix[0][0] * matrix[1][1] - matrix[0][1] * matrix[1][0]
+    second = (vector[0] * matrix[1][1] - vector[1] * matrix[1][0]) / determinant
+    third = (vector[1] * matrix[0][0] - vector[0] * matrix[0][1]) / determinant
+    which = task(lax.broadcasted_iota(jnp.int32, (32, 1), 0))
+    return jnp.where(which == 0, 1.0 - second - third, jnp.where(which == 1, second, third))
+
+
+def slope(x):
+    s = 1.0 / (1.0 + jnp.exp(-x))
+    return s * (1.0 + x * (1.0 - s))
+
+
+def pyramid(trunk, weight, affine, heads, targets, square, *refs):
+    (full, predictions, head_grad, sums, other) = refs[:5]
+    refs = refs[1:]
+    (wide, sides, own, out, near, cross, hidden, pre, grad, branch) = refs[4:14]
+    (s_send, s_ch, s_mid, s_pix, b_send, b_ch, b_mid, b_pix) = refs[14:22]
+    (h_send, h_ch, h_mid, h_pix, h_sum, p_send, p_ch) = refs[22:29]
+    (w_sems, near_sems, far_sems, ch_sems, pix_sems, g_near, g_far, g_hop, y_sems) = refs[29:]
+    p, c = lax.axis_index("pix"), lax.axis_index("ch")
+    k, x = lax.rem(c, 2), c // 2
+    m = weight.shape[4]
+    quarter = targets.shape[0] // SPLIT
+    barrier, expected = greet((1, 2, 3), FAR_FIRST)
+    loads = load_pyramid(weight, wide, w_sems)
+    contract0 = (((0,), (0,)), ((), ()))
+    contract1 = (((1,), (1,)), ((), ()))
+    head = heads[...]
+    scaled = head * task_vector(
+        add_up(square, PHASES)[:, :32], lax.dot_general(head, head, contract1, precision=highest)
+    )
+    mine = rows(c * quarter, quarter)
+    target, mask = targets[mine, :32], targets[mine, 32:33]
+    grad[...] = jnp.dot(target, scaled, precision=highest) * mask
+    pl.semaphore_wait(barrier, expected)
+    to_other = push(trunk, other, y_sems.at[0], y_sems.at[1], (p ^ 1, c))
+
+    copies = []
+    for j in range(3):
+        s, q = RATE_ROWS[j] * 32, RATE_COLS[j]
+        for a in (1, 0, 2):
+            for load in loads[3 * j + a]:
+                load.wait()
+            if a == 1:
+                sides[...] = jnp.dot(trunk[...], wide[3 * j + 1], preferred_element_type=f32)
+            elif a == 0:
+                sides[s:] += jnp.dot(trunk[: 1024 - s], wide[3 * j], preferred_element_type=f32)
+            else:
+                sides[: 1024 - s] += jnp.dot(trunk[s:], wide[3 * j + 2], preferred_element_type=f32)
+        for d in range(SPLIT):
+            at = slice(d * quarter, (d + 1) * quarter)
+            value = (
+                sides[at, m : 2 * m]
+                + move_cols(sides[at, :m], q)
+                + move_cols(sides[at, 2 * m :], -q)
+            )
+            own[d, j] = value
+            out[d, j] = value.astype(bf16)
+        copies.append(
+            [
+                push(out.at[2 * h + 1 - k, j], near.at[h, j], near_sems.at[0, j, h], near_sems.at[1, j, h], (p, c ^ 1))
+                for h in range(2)
+            ]
+        )
+        if j > 0:
+            copies[j - 1] = cross_chips(copies[j - 1], j - 1, own, near, cross, far_sems)
+    copies[2] = cross_chips(copies[2], 2, own, near, cross, far_sems)
+    count = total(jnp.broadcast_to(mask, (quarter, 128)))[:, :1]
+    for j in range(3):
+        copies[j].wait()
+        value = own[2 * x + k, j] + near[x, j].astype(f32) + cross[1, j].astype(f32)
+        at = slice(j * m, (j + 1) * m)
+        hidden[:, at] = value
+        first = total(value * mask)
+        apart = value - first / jnp.maximum(count, 1.0)
+        s_send[j : j + 1] = first
+        s_send[3 + j : 4 + j] = total(apart * apart * mask)
+    s_send[6:7] = jnp.broadcast_to(count, (1, m))
+    s_send[7:8] = jnp.zeros((1, m), f32)
+
+    def merge(recv, parts):
+        number = recv[0, 6:7]
+        for i in range(1, parts):
+            number = number + recv[i, 6:7]
+        whole, spread = recv[0, 0:3], recv[0, 3:6]
+        for i in range(1, parts):
+            whole, spread = whole + recv[i, 0:3], spread + recv[i, 3:6]
+        center = whole / jnp.maximum(number, 1.0)
+        for i in range(parts):
+            n = recv[i, 6:7]
+            apart = recv[i, 0:3] / jnp.maximum(n, 1.0) - center
+            spread = spread + n * apart * apart
+        return whole, spread, number
+
+    ch_exchange(s_send, s_ch, ch_sems.at[0])
+    whole, spread, number = merge(s_ch, SPLIT)
+    s_mid[0:3] = whole
+    s_mid[3:6] = spread
+    s_mid[6:7] = number
+    s_mid[7:8] = jnp.zeros((1, m), f32)
+    pix_exchange(s_mid, s_pix, pix_sems.at[0])
+    whole, spread, number = merge(s_pix, PHASES)
+    center, scale = whole / number, lax.rsqrt(spread / number + epsilon)
+    for j in range(3):
+        at = slice(j * m, (j + 1) * m)
+        norm = (hidden[:, at] - center[j : j + 1]) * scale[j : j + 1]
+        hidden[:, at] = norm
+        value = norm * affine[0:1, at] + affine[1:2, at]
+        branch[:, at] = (silu(value) * mask).astype(bf16)
+        back = grad[:, at] * slope(value)
+        grad[:, at] = back
+        b_send[j : j + 1] = total(back)
+        b_send[3 + j : 4 + j] = total(back * norm)
+    b_send[6:8] = jnp.zeros((2, m), f32)
+    p_send[...] = lax.dot_general(
+        head.astype(bf16), branch[...], contract1, preferred_element_type=f32
+    )
+    h_send[...] = lax.dot_general(
+        target, branch[...].astype(f32), contract0, precision=highest, preferred_element_type=f32
+    )
+    background = [
+        [push(p_send, p_ch.at[c], ch_sems.at[1, 0, i], ch_sems.at[1, 1, i], (p, c ^ i)) for i in (2, 3, 1)],
+        [
+            push(h_send.at[rows((c ^ i) * 8, 8)], h_ch.at[c], ch_sems.at[2, 0, i], ch_sems.at[2, 1, i], (p, c ^ i))
+            for i in (2, 3, 1)
+        ],
+    ]
+    p_ch[c] = p_send[...]
+    h_ch[c] = h_send[rows(c * 8, 8)]
+    ch_exchange(b_send, b_ch, ch_sems.at[3])
+    b_mid[...] = add_up(b_ch, SPLIT)
+    for copy in background[0] + background[1]:
+        copy.wait()
+    h_mid[...] = add_up(h_ch, SPLIT)
+    sending = [
+        push(b_mid, b_pix.at[p], pix_sems.at[1, 0, i], pix_sems.at[1, 1, i], (p ^ i, c)) for i in FAR_FIRST
+    ]
+    b_pix[p] = b_mid[...]
+
+    def half(to):
+        return p_ch.at[to // 2, :, rows(lax.rem(to, 2) * 128, 128)]
+
+    background = [
+        push(half(p ^ i), predictions.at[p], pix_sems.at[2, 0, i], pix_sems.at[2, 1, i], (p ^ i, c)) for i in FAR_FIRST
+    ] + [push(h_mid, h_pix.at[p], pix_sems.at[3, 0, i], pix_sems.at[3, 1, i], (p ^ i, c)) for i in FAR_FIRST]
+    predictions[p] = half(p)[...]
+    h_pix[p] = h_mid[...]
+    for copy in sending:
+        copy.wait()
+    summed = add_up(b_pix, PHASES)
+    sums[...] = summed
+    for j in range(3):
+        at = slice(j * m, (j + 1) * m)
+        value = grad[:, at] - mask * (summed[j : j + 1] + hidden[:, at] * summed[3 + j : 4 + j]) / number
+        full[mine, at] = (affine[0:1, at] * scale[j : j + 1] * value).astype(bf16)
+    far = push(full.at[mine], full.at[mine], g_far.at[0], g_far.at[1], (p, c ^ 2))
+    by = push(full.at[mine], full.at[mine], g_near.at[0], g_near.at[1], (p, c ^ 1))
+    for copy in background:
+        copy.wait()
+    own_rows = add_up(h_pix, PHASES)
+    h_sum[...] = own_rows
+    head_grad[rows(c * 8, 8)] = own_rows
+    last = [
+        push(h_sum, head_grad.at[rows(c * 8, 8)], ch_sems.at[4, 0, i], ch_sems.at[4, 1, i], (p, c ^ i))
+        for i in (2, 3, 1)
+    ]
+    far.wait_recv()
+    theirs = rows((c ^ 2) * quarter, quarter)
+    hop = push(full.at[theirs], full.at[theirs], g_hop.at[0], g_hop.at[1], (p, c ^ 1))
+    far.wait_send()
+    by.wait()
+    hop.wait()
+    for copy in last:
+        copy.wait()
+    to_other.wait()
+
+
+def cross_chips(near_copies, j, own, near, cross, sems):
+    p, c = lax.axis_index("pix"), lax.axis_index("ch")
+    k, x = lax.rem(c, 2), c // 2
+    for copy in near_copies:
+        copy.wait()
+    cross[0, j] = (own[2 * (1 - x) + k, j] + near[1 - x, j].astype(f32)).astype(bf16)
+    return push(cross.at[0, j], cross.at[1, j], sems.at[0, j], sems.at[1, j], (p, c ^ 2))
+
+
+def run_pyramid(cid, trunk, weight, affine, heads, targets, square):
+    pixels, n = trunk.shape
+    m = weight.shape[4]
+    quarter = pixels // SPLIT
+    outs = [
+        shape((pixels, 3 * m), bf16),
+        shape((PHASES, 32, 128), f32),
+        shape((32, 3 * m), f32),
+        shape((8, m), f32),
+        shape((pixels, n), bf16),
+    ]
+    small = [pltpu.VMEM((8, m), f32), pltpu.VMEM((SPLIT, 8, m), f32), pltpu.VMEM((8, m), f32), pltpu.VMEM((PHASES, 8, m), f32)]
+    scratch = (
+        [
+            pltpu.VMEM((9, n, 3 * m), bf16),
+            pltpu.VMEM((pixels, 3 * m), f32),
+            pltpu.VMEM((SPLIT, 3, quarter, m), f32),
+            pltpu.VMEM((SPLIT, 3, quarter, m), bf16),
+            pltpu.VMEM((2, 3, quarter, m), bf16),
+            pltpu.VMEM((2, 3, quarter, m), bf16),
+            pltpu.VMEM((quarter, 3 * m), f32),
+            pltpu.VMEM((8, 128), f32),
+            pltpu.VMEM((quarter, 3 * m), f32),
+            pltpu.VMEM((quarter, 3 * m), bf16),
+        ]
+        + small
+        + small
+        + [
+            pltpu.VMEM((32, 3 * m), f32),
+            pltpu.VMEM((SPLIT, 8, 3 * m), f32),
+            pltpu.VMEM((8, 3 * m), f32),
+            pltpu.VMEM((PHASES, 8, 3 * m), f32),
+            pltpu.VMEM((8, 3 * m), f32),
+            pltpu.VMEM((32, quarter), f32),
+            pltpu.VMEM((SPLIT, 32, quarter), f32),
+        ]
+        + [dma(9, 3), dma(2, 3, 2), dma(2, 3), dma(5, 2, SPLIT), dma(4, 2, PHASES), dma(2), dma(2), dma(2), dma(2)]
+    )
+    vmem = pl.BlockSpec(memory_space=pltpu.VMEM)
+    specs = [vmem] * 6
+    specs[1] = pl.BlockSpec(memory_space=pl.ANY)
+    return pl.pallas_call(
+        pyramid,
+        out_shape=outs,
+        in_specs=specs,
+        out_specs=[vmem] * len(outs),
+        scratch_shapes=scratch,
+        compiler_params=pltpu.CompilerParams(
+            collective_id=cid, has_side_effects=True, vmem_limit_bytes=VMEM_BYTES
+        ),
+        name="pyramid",
+    )(trunk, weight, affine, heads, targets, square)
+
+
+def packed_sums(values, send):
+    i = 0
+    for value in values:
+        for g in range(value.shape[1] // 128):
+            send[i : i + 1] = value[:, g * 128 : (g + 1) * 128]
+            i += 1
+
+
+def unpacked_sums(recv, rows_each, count):
+    out, i = [], 0
+    for _ in range(count):
+        parts = []
+        for _ in range(rows_each):
+            value = recv[0, i : i + 1]
+            for d in range(1, PHASES):
+                value = value + recv[d, i : i + 1]
+            parts.append(value)
+            i += 1
+        out.append(parts[0] if rows_each == 1 else jnp.concatenate(parts, axis=1))
+    return out
+
+
+def spread_lanes(v, n):
+    return v if n == 128 else jnp.concatenate([v] * (n // 128), axis=1)
+
+
+def backward(
+    grads, trunk, other, weight, norm3, masked, valid, expand, affine3, norm2, affine2, full2, taps, dilated,
+    norm1, affine1, reduce_rows, stats1, stats2, stats3, *refs
+):
+    outs, scratch = refs[:8], refs[8:]
+    (features_grad, aspp_parts, dilated_grad, expand_grad, reduce_grad, sums3_out, sums2_out, sums1_out) = outs
+    (wide, moved, acc, dsend, drecv, tpad, picked, picked_in, turned, zsend, zown) = scratch[:11]
+    (gp3, g3, own, out, near, cross, hidden, gp2, g2, prod, edges, g1) = scratch[11:23]
+    gp1, lanes = gp2, own
+    (st3, st3r, st2, st2r, st1, st1r, e_part, e_mid, e_sum, d_part, d_sum, r_part, r_mid, r_sum) = scratch[23:37]
+    (w_sems, d_sems, y_sems, z_sems, near_sems, far_sems, st_sems, gn, gf, gh, gn1, gf1, gh1, edge_sems, ch_sems, pix_sems, own_sems) = scratch[37:]
+    p, c = lax.axis_index("pix"), lax.axis_index("ch")
+    y, z = lax.rem(p, 2), p // 2
+    pixels, n = norm3.shape
+    m = weight.shape[4]
+    mid = norm2.shape[1]
+    tile = pixels // TILES
+    contract0 = (((0,), (0,)), ((), ()))
+    contract1 = (((1,), (1,)), ((), ()))
+    count = stats1[2:3, :1]
+    barrier, expected = greet((1, 2, 3), FAR_FIRST)
+    loads = load_pyramid(weight, wide, w_sems)
+
+    row = lax.broadcasted_iota(jnp.int32, (m, m), 0)
+    col = lax.broadcasted_iota(jnp.int32, (m, m), 1)
+    source = (2 * ((col % 128) // 32) + col // 128) * 32 + col % 32
+    pick = jnp.where(row == source, 1.0, 0.0).astype(bf16)
+    for j in range(3):
+        value = jnp.dot(grads[:, j * m : (j + 1) * m], pick, preferred_element_type=f32).astype(bf16)
+        picked[0, j] = value[:, :128]
+        picked[1, j] = value[:, 128:]
+    pl.semaphore_wait(barrier, expected)
+    sent_picks = push(picked.at[1 - y], picked_in, y_sems.at[0], y_sems.at[1], (p ^ 1, c))
+
+    for j in range(3):
+        q = RATE_COLS[j]
+        plain = grads[:, j * m : (j + 1) * m]
+        value = plain.astype(f32)
+        moved[j, :, :m] = move_cols(value, -q).astype(bf16)
+        moved[j, :, m : 2 * m] = plain
+        moved[j, :, 2 * m :] = move_cols(value, q).astype(bf16)
+    back = []
+    for h in range(2):
+        half = slice(h * m, (h + 1) * m)
+        for j in range(3):
+            s = RATE_ROWS[j] * 32
+            for a in (1, 0, 2):
+                if h == 0:
+                    for load in loads[3 * j + a]:
+                        load.wait()
+                w = wide[3 * j + a, half]
+                if a == 1:
+                    value = lax.dot_general(moved[j], w, contract1, preferred_element_type=f32)
+                    if j == 0:
+                        acc[...] = value
+                    else:
+                        acc[...] += value
+                elif a == 0:
+                    acc[: pixels - s] += lax.dot_general(moved[j, s:], w, contract1, preferred_element_type=f32)
+                else:
+                    acc[s:] += lax.dot_general(moved[j, : pixels - s], w, contract1, preferred_element_type=f32)
+        dsend[h] = acc[...].astype(bf16)
+        for k in FAR_FIRST:
+            back.append(
+                push(
+                    dsend.at[h, rows((p ^ k) * 128, 128)],
+                    drecv.at[h, rows(p * 128, 128)],
+                    d_sems.at[0, h, k],
+                    d_sems.at[1, h, k],
+                    (p ^ k, c),
+                )
+            )
+        back.append(keep(dsend.at[h, rows(p * 128, 128)], drecv.at[h, rows(p * 128, 128)], own_sems.at[h]))
+
+    for i, source in enumerate((trunk, other)):
+        tpad[i, :64] = jnp.zeros((64, n), bf16)
+        tpad[i, 64 : 64 + pixels] = source[...]
+        tpad[i, 64 + pixels :] = jnp.zeros((64, n), bf16)
+
+    def turn(i, part):
+        at = slice(i * pixels, (i + 1) * pixels)
+        for j in range(3):
+            q = RATE_COLS[j]
+            plain = part(j)
+            value = plain.astype(f32)
+            for b, piece in enumerate((move_cols(value, -q).astype(bf16), plain, move_cols(value, q).astype(bf16))):
+                turned[j, b * 128 : (b + 1) * 128, at] = piece.T
+
+    turn(0, lambda j: picked[y, j])
+    sent_picks.wait()
+    turn(1, lambda j: picked_in[j])
+    for j in range(3):
+        s = RATE_ROWS[j] * 32
+        for a in range(3):
+            if a == 1:
+                low, high, start = 0, pixels, 64
+            elif a == 0:
+                low, high = s // 128 * 128, pixels
+                start = 64 + low - s
+            else:
+                low, high, start = 0, -(-(pixels - s) // 128) * 128, 64 + s
+            value = None
+            for i in range(2):
+                term = jnp.dot(
+                    turned[j, :, i * pixels + low : i * pixels + high],
+                    tpad[i, start : start + high - low],
+                    preferred_element_type=f32,
+                )
+                value = term if value is None else value + term
+            value = value.astype(bf16)
+            for b in range(3):
+                for to in range(4):
+                    at = b * 128 + to * 32
+                    zsend[to, (3 * j + a) * 3 + b] = value[at : at + 32]
+    for copy in back:
+        copy.wait()
+    zcopies = [
+        push(zsend.at[z ^ k], aspp_parts.at[z], z_sems.at[0, k], z_sems.at[1, k], (p ^ (2 * k), c)) for k in (3, 2, 1)
+    ]
+    zcopies.append(keep(zsend.at[z], aspp_parts.at[z], own_sems.at[2]))
+
+    def norm_back(grad, norm, sums, scale, gain, v):
+        return gain * scale * (grad - v * (sums[0] + norm * sums[1]) / count)
+
+    def three(i, carry):
+        at = rows(i * 32, 32)
+        norm = norm3[at]
+        pre = norm * affine3[0:1] + affine3[1:2] + masked[at].astype(f32)
+        grad = jnp.concatenate([drecv[0, at], drecv[1, at]], axis=1).astype(f32)
+        grad = grad * spread_lanes(valid[at], n) * slope(pre)
+        gp3[at] = grad
+        return carry[0] + fold(grad), carry[1] + fold(grad * norm)
+
+    zero = jnp.zeros((8, n), f32)
+    bias, gain = loop(pixels // 32, three, (zero, zero))
+    packed_sums((total(bias), total(gain)), st3)
+    pix_exchange(st3, st3r, st_sems.at[0])
+    sums = unpacked_sums(st3r, n // 128, 2)
+    sums3_out[0:1] = sums[0]
+    sums3_out[1:2] = sums[1]
+
+    def part3(t):
+        def step(i, carry):
+            at = rows(t * tile + i * 32, 32)
+            v = spread_lanes(valid[at], n)
+            g3[at] = norm_back(gp3[at], norm3[at], sums, stats3[1:2], affine3[0:1], v).astype(bf16)
+            return carry
+
+        loop(tile // 32, step, 0)
+        return lax.dot_general(g3[t * tile : (t + 1) * tile], expand[...], contract1, preferred_element_type=f32)
+
+    result = sum_over_ch(part3, tile, TILES, own, out, near, cross, near_sems.at[0], far_sems.at[0])
+    value = lax.dot_general(full2[...], g3[...], contract0, preferred_element_type=f32).astype(bf16)
+    for d in range(SPLIT):
+        e_part[d] = value[d * mid : (d + 1) * mid]
+    e_copies = [
+        push(e_part.at[c ^ k], e_mid.at[c], ch_sems.at[0, 0, k], ch_sems.at[0, 1, k], (p, c ^ k)) for k in (2, 3, 1)
+    ]
+    e_copies.append(keep(e_part.at[c], e_mid.at[c], own_sems.at[3]))
+
+    bias, gain = jnp.zeros((8, mid), f32), jnp.zeros((8, mid), f32)
+    for t in range(TILES):
+        hidden[t * tile : (t + 1) * tile] = result(t)
+
+    def two(i, carry):
+        at = rows(i * 128, 128)
+        norm = norm2[at]
+        grad = hidden[at] * valid[at] * slope(norm * affine2[0:1] + affine2[1:2])
+        gp2[at] = grad
+        return carry[0] + fold(grad), carry[1] + fold(grad * norm)
+
+    bias, gain = loop(pixels // 128, two, (bias, gain))
+    packed_sums((total(bias), total(gain)), st2)
+    pix_exchange(st2, st2r, st_sems.at[1])
+    sums2 = unpacked_sums(st2r, 1, 2)
+    sums2_out[0:1] = sums2[0]
+    sums2_out[1:2] = sums2[1]
+
+    def ready2(t):
+        def step(i, carry):
+            at = rows(t * tile + i * 128, 128)
+            value = norm_back(gp2[at], norm2[at], sums2, stats2[1:2], affine2[0:1], valid[at])
+            g2[at, rows(c * mid, mid)] = value.astype(bf16)
+            return carry
+
+        loop(tile // 128, step, 0)
+
+    gather_over_ch(g2, mid, tile, TILES, gn, gf, gh, ready2)
+    for t in range(TILES):
+        at = pl.ds(t * tile, tile)
+        prod[at] = lax.dot_general(g2[at], dilated[...], contract1, preferred_element_type=f32)
+
+    place = lax.broadcasted_iota(jnp.int32, (128, mid), 0) % 32
+
+    def across(i, a):
+        beta = i % COL_CLASSES
+        two_on = (i - beta + (beta + 2) % 4) * 128
+        here = slice(i * 128, (i + 1) * 128)
+        there = slice(two_on, two_on + 128)
+        lane = lambda b: slice((3 * a + b) * mid, (3 * a + b + 1) * mid)
+        left, right = prod[there, lane(0)], prod[there, lane(2)]
+        if beta >= 2:
+            left = jnp.where(place == 31, 0.0, pltpu.roll(left, 127, 0))
+        else:
+            right = jnp.where(place == 0, 0.0, pltpu.roll(right, 1, 0))
+        return prod[here, lane(1)] + left + right
+
+    for i in range(PHASES):
+        at = slice(i * 128, (i + 1) * 128)
+        up, same, down = across(i, 0), across(i, 1), across(i, 2)
+        zero = jnp.zeros((32, mid), f32)
+        hidden[at] = same + jnp.concatenate([up[32:], zero]) + jnp.concatenate([zero, down[:96]])
+        edges[0, i] = up[:32].astype(bf16)
+        edges[1, i] = down[96:].astype(bf16)
+    first, last = p == 0, p == PHASES - 1
+    to_next = lambda: pltpu.make_async_remote_copy(
+        src_ref=edges.at[1], dst_ref=edges.at[2], send_sem=edge_sems.at[0, 0], recv_sem=edge_sems.at[1, 0],
+        device_id=(p + 1, c), device_id_type=MESH,
+    )
+    to_last = lambda: pltpu.make_async_remote_copy(
+        src_ref=edges.at[0], dst_ref=edges.at[3], send_sem=edge_sems.at[0, 1], recv_sem=edge_sems.at[1, 1],
+        device_id=(p - 1, c), device_id_type=MESH,
+    )
+
+    @pl.when(jnp.logical_not(last))
+    def _():
+        to_next().start()
+
+    @pl.when(jnp.logical_not(first))
+    def _():
+        to_last().start()
+
+    @pl.when(first)
+    def _():
+        edges[2] = jnp.zeros((PHASES, 32, mid), bf16)
+
+    @pl.when(last)
+    def _():
+        edges[3] = jnp.zeros((PHASES, 32, mid), bf16)
+
+    value = lax.dot_general(g2[...], taps[...], contract0, preferred_element_type=f32).astype(bf16)
+    out_rows = SPLIT * mid // PHASES
+    for d in range(PHASES):
+        d_part[d] = value[d * out_rows : (d + 1) * out_rows]
+
+    @pl.when(jnp.logical_not(last))
+    def _():
+        to_next().wait_send()
+        to_last().wait_recv()
+
+    @pl.when(jnp.logical_not(first))
+    def _():
+        to_last().wait_send()
+        to_next().wait_recv()
+
+    bias, gain = jnp.zeros((8, mid), f32), jnp.zeros((8, mid), f32)
+    for i in range(PHASES):
+        at = slice(i * 128, (i + 1) * 128)
+        zero = jnp.zeros((64, mid), f32)
+        edge = jnp.concatenate([edges[2, i].astype(f32), zero, edges[3, i].astype(f32)])
+        norm = norm1[at]
+        grad = (hidden[at] + edge) * valid[at] * slope(norm * affine1[0:1] + affine1[1:2])
+        gp1[at] = grad
+        bias, gain = bias + fold(grad), gain + fold(grad * norm)
+    packed_sums((total(bias), total(gain)), st1)
+    pix_exchange(st1, st1r, st_sems.at[2])
+    sums1 = unpacked_sums(st1r, 1, 2)
+    sums1_out[0:1] = sums1[0]
+    sums1_out[1:2] = sums1[1]
+
+    def ready1(t):
+        def step(i, carry):
+            at = rows(t * tile + i * 128, 128)
+            value = norm_back(gp1[at], norm1[at], sums1, stats1[1:2], affine1[0:1], valid[at])
+            g1[at, rows(c * mid, mid)] = value.astype(bf16)
+            return carry
+
+        loop(tile // 128, step, 0)
+
+    gather_over_ch(g1, mid, tile, TILES, gn1, gf1, gh1, ready1)
+    value = lax.dot_general(masked[...], g1[...], contract0, preferred_element_type=f32).astype(bf16)
+    for d in range(SPLIT):
+        r_part[d] = value[:, d * mid : (d + 1) * mid]
+    r_copies = [
+        push(r_part.at[c ^ k], r_mid.at[rows(c * n, n)], ch_sems.at[1, 0, k], ch_sems.at[1, 1, k], (p, c ^ k))
+        for k in (2, 3, 1)
+    ]
+    r_copies.append(keep(r_part.at[c], r_mid.at[rows(c * n, n)], own_sems.at[4]))
+    for copy in e_copies:
+        copy.wait()
+
+    def wanted(to):
+        return e_mid.at[to // 2, :, rows(lax.rem(to, 2) * 256, 256)]
+
+    pix_copies = [
+        push(wanted(p ^ k), e_sum.at[p], pix_sems.at[0, 0, k], pix_sems.at[0, 1, k], (p ^ k, c)) for k in FAR_FIRST
+    ]
+    pix_copies.append(keep(wanted(p), e_sum.at[p], own_sems.at[5]))
+    pix_copies += [
+        push(d_part.at[p ^ k], d_sum.at[p], pix_sems.at[1, 0, k], pix_sems.at[1, 1, k], (p ^ k, c)) for k in FAR_FIRST
+    ]
+    pix_copies.append(keep(d_part.at[p], d_sum.at[p], own_sems.at[6]))
+    for copy in r_copies:
+        copy.wait()
+    pix_copies += [
+        push(r_mid.at[rows((p ^ k) * 256, 256)], r_sum.at[p], pix_sems.at[2, 0, k], pix_sems.at[2, 1, k], (p ^ k, c))
+        for k in FAR_FIRST
+    ]
+    pix_copies.append(keep(r_mid.at[rows(p * 256, 256)], r_sum.at[p], own_sems.at[7]))
+
+    for i in range(PHASES):
+        at = slice(i * 128, (i + 1) * 128)
+        value = lax.dot_general(g1[at], reduce_rows[...], contract1, preferred_element_type=f32) + gp3[at]
+        value = value * spread_lanes(valid[at], n)
+        for g in range(n // 128):
+            for r in range(4):
+                start = (2 * r + i // COL_CLASSES) * 128 + i % COL_CLASSES
+                lanes[g, pl.ds(start, 32, stride=COL_CLASSES), :] = value[r * 32 : (r + 1) * 32, g * 128 : (g + 1) * 128]
+    for g in range(n // 128):
+        features_grad[:, g * 128 : (g + 1) * 128] = lanes[g].astype(bf16)
+    for copy in pix_copies:
+        copy.wait()
+
+    def gathered(parts):
+        value = parts[0].astype(f32)
+        for d in range(1, PHASES):
+            value = value + parts[d].astype(f32)
+        return value
+
+    expand_grad[...] = gathered(e_sum)
+    reduce_grad[...] = gathered(r_sum)
+    dilated_grad[...] = gathered(d_sum)
+    for copy in zcopies:
+        copy.wait()
+    del zown
+
+
+def run_backward(cid, arrays):
+    (grads, trunk, other, weight, norm3, masked, valid, expand, affine3, norm2, affine2, full2, taps, dilated,
+     norm1, affine1, reduce_rows, stats1, stats2, stats3) = arrays
+    pixels, n = norm3.shape
+    m = weight.shape[4]
+    mid = norm2.shape[1]
+    all_mid = SPLIT * mid
+    outs = [
+        shape((pixels, n), bf16),
+        shape((4, 27, 32, n), bf16),
+        shape((all_mid // PHASES, 9 * mid), f32),
+        shape((mid, 256), f32),
+        shape((256, mid), f32),
+        shape((8, n), f32),
+        shape((8, mid), f32),
+        shape((8, mid), f32),
+    ]
+    sums = sum_scratch(pixels, mid, TILES)
+    scratch = [
+        pltpu.VMEM((9, n, 3 * m), bf16),
+        pltpu.VMEM((3, pixels, 3 * m), bf16),
+        pltpu.VMEM((pixels, m), f32),
+        pltpu.VMEM((2, pixels, m), bf16),
+        pltpu.VMEM((2, pixels, m), bf16),
+        pltpu.VMEM((2, pixels + 128, n), bf16),
+        pltpu.VMEM((2, 3, pixels, 128), bf16),
+        pltpu.VMEM((3, pixels, 128), bf16),
+        pltpu.VMEM((3, 384, 2 * pixels), bf16),
+        pltpu.VMEM((4, 27, 32, n), bf16),
+        pltpu.VMEM((8, 128), f32),
+        pltpu.VMEM((pixels, n), f32),
+        pltpu.VMEM((pixels, n), bf16),
+        *sums[:4],
+        pltpu.VMEM((pixels, mid), f32),
+        pltpu.VMEM((pixels, mid), f32),
+        pltpu.VMEM((pixels, all_mid), bf16),
+        pltpu.VMEM((pixels, 9 * mid), f32),
+        pltpu.VMEM((4, PHASES, 32, mid), bf16),
+        pltpu.VMEM((pixels, all_mid), bf16),
+        pltpu.VMEM((8, 128), f32),
+        pltpu.VMEM((PHASES, 8, 128), f32),
+        pltpu.VMEM((8, 128), f32),
+        pltpu.VMEM((PHASES, 8, 128), f32),
+        pltpu.VMEM((8, 128), f32),
+        pltpu.VMEM((PHASES, 8, 128), f32),
+        pltpu.VMEM((SPLIT, mid, n), bf16),
+        pltpu.VMEM((SPLIT, mid, n), bf16),
+        pltpu.VMEM((PHASES, mid, 256), bf16),
+        pltpu.VMEM((PHASES, all_mid // PHASES, 9 * mid), bf16),
+        pltpu.VMEM((PHASES, all_mid // PHASES, 9 * mid), bf16),
+        pltpu.VMEM((SPLIT, n, mid), bf16),
+        pltpu.VMEM((SPLIT * n, mid), bf16),
+        pltpu.VMEM((PHASES, 256, mid), bf16),
+        dma(9, 3),
+        dma(2, 2, PHASES),
+        dma(2),
+        dma(2, 4),
+        dma(1, 2, TILES, 2),
+        dma(1, 2, TILES),
+        dma(3, 2, PHASES),
+        *gather_scratch(TILES),
+        *gather_scratch(TILES),
+        dma(2, 2),
+        dma(2, 2, SPLIT),
+        dma(3, 2, PHASES),
+        dma(8),
+    ]
+    vmem = pl.BlockSpec(memory_space=pltpu.VMEM)
+    specs = [vmem] * len(arrays)
+    specs[3] = pl.BlockSpec(memory_space=pl.ANY)
+    return pl.pallas_call(
+        backward,
+        out_shape=outs,
+        in_specs=specs,
+        out_specs=[vmem, pl.BlockSpec(memory_space=pl.ANY)] + [vmem] * (len(outs) - 2),
+        scratch_shapes=scratch,
+        compiler_params=pltpu.CompilerParams(
+            collective_id=cid, has_side_effects=True, vmem_limit_bytes=VMEM_BYTES
+        ),
+        name="backward",
+    )(*arrays)
+
+
+def finish_pyramid(parts, result):
+    value = parts[0, 0].astype(f32)
+    for i in range(1, 4):
+        value = value + parts[i, 0].astype(f32)
+    result[0] = value.T
+
+
+def run_finish(parts):
+    steps, n = parts.shape[1], parts.shape[3]
+    return pl.pallas_call(
+        finish_pyramid,
+        grid=(steps,),
+        out_shape=shape((steps, n, 32), f32),
+        in_specs=[pl.BlockSpec((4, 1, 32, n), lambda i: (0, i, 0, 0))],
+        out_specs=pl.BlockSpec((1, n, 32), lambda i: (i, 0, 0)),
+        name="finish_pyramid",
+    )(parts)
+
+
+def fast_device(
+    features,
+    pixel_mask,
+    reduce_weight,
+    reduce_gain,
+    reduce_bias,
+    dilated_weight,
+    dilated_gain,
+    dilated_bias,
+    expand_weight,
+    expand_gain,
+    expand_bias,
+    aspp_weight,
+    aspp_gain,
+    aspp_bias,
+    task_weight,
+    cotangent,
+):
+    rows_here, width, local_in = features.shape
+    pixels = rows_here * width
+    local_mid = reduce_weight.shape[1]
+    full_mid = dilated_weight.shape[3]
+    branch_width = aspp_weight.shape[4]
+    own_branch = task_weight.shape[1]
+    outs_count = task_weight.shape[2]
+    me_ch = lax.axis_index("ch")
+    quarter = pixels // 4
+    valid = to_classes(pixel_mask.astype(f32).reshape(rows_here, width, 1)).reshape(pixels, 1)
+    valid_wide = jnp.broadcast_to(valid, (pixels, 128))
+    heads = jnp.concatenate(
+        [
+            task_weight.astype(f32).transpose(2, 0, 1).reshape(outs_count, -1),
+            jnp.zeros((32 - outs_count, 3 * own_branch), f32),
+            aspp_gain.reshape(1, -1),
+            aspp_bias.reshape(1, -1),
+            jnp.zeros((6, 3 * own_branch), f32),
+        ]
+    )
+    heads = jnp.pad(heads, ((0, 0), (0, 256 - 3 * own_branch)))
+    target_here = jnp.concatenate(
+        [
+            to_classes(cotangent).reshape(pixels, outs_count) * valid,
+            jnp.zeros((pixels, 32 - outs_count), f32),
+            valid_wide[:, :96],
+        ],
+        axis=1,
+    )
+    square = jnp.einsum("po,pq->oq", target_here[:, :32], target_here[:, :32], precision=highest)
+    square = jnp.pad(square, ((0, 0), (0, 96)))
+
+    def affine(gain, bias):
+        return jnp.concatenate([gain[None], bias[None], jnp.zeros((6, gain.shape[0]), f32)])
+
+    masked, reduce_rows, expand_cols, heads_all, target_class, square_all, norm_one, padded_one, stat_one = run_stage_one(
+        1,
+        features.reshape(pixels, local_in),
+        valid_wide,
+        reduce_weight,
+        expand_weight,
+        affine(reduce_gain, reduce_bias),
+        heads,
+        target_here.reshape(PHASES, -1, 128),
+        square,
+    )
+    heads_all = (
+        heads_all[:, :, : 3 * own_branch]
+        .reshape(4, heads.shape[0], 3, own_branch)
+        .transpose(1, 2, 0, 3)
+        .reshape(heads.shape[0], 3 * branch_width)
+    )
+    head_weight, branch_gain, branch_bias = heads_all[:32], heads_all[32:33], heads_all[33:34]
+    target_class = target_class.reshape(pixels, 128)
+
+    norm_two, act_two_full, taps_one, stat_two = run_stage_two(
+        2, padded_one, valid_wide, dilated_weight.reshape(9 * local_mid, full_mid), affine(dilated_gain, dilated_bias)
+    )
+    norm_three, trunk_class, stat_three = run_stage_three(
+        3, act_two_full, expand_cols, masked, valid_wide, affine(expand_gain, expand_bias)
+    )
+    grad_full, predictions, head_grad, branch_sums, trunk_other = run_pyramid(
+        4, trunk_class, aspp_weight, heads_all[32:40], head_weight, target_class, square_all
+    )
+    predictions = from_classes(predictions.transpose(0, 2, 1), rows_here, width)[:, :, :outs_count]
+    head_grad = head_grad.reshape(32, 3, 4, own_branch).transpose(2, 1, 3, 0)
+    task_weight_grad = lax.dynamic_index_in_dim(head_grad, me_ch, keepdims=False)[:, :, :outs_count]
+    own_sums = lax.dynamic_slice_in_dim(
+        branch_sums[:6].reshape(2, 3, branch_width), me_ch * own_branch, own_branch, axis=2
+    )
+    aspp_bias_grad, aspp_gain_grad = own_sums[0], own_sums[1]
+    dilated_rows = dilated_weight.reshape(9 * local_mid, full_mid)
+    features_grad, aspp_parts, dilated_sum, expand_weight_grad, reduce_weight_grad, sums3, sums2, sums1 = run_backward(
+        5,
+        [
+            grad_full, trunk_class, trunk_other, aspp_weight, norm_three, masked, valid_wide, expand_cols,
+            affine(expand_gain, expand_bias), norm_two, affine(dilated_gain, dilated_bias), act_two_full, taps_one,
+            dilated_rows, norm_one, affine(reduce_gain, reduce_bias), reduce_rows, stat_one, stat_two, stat_three,
+        ],
+    )
+    features_grad = features_grad.reshape(rows_here, width, local_in)
+    aspp_weight_grad = run_finish(aspp_parts).reshape(3, 3, 3, local_in, -1)
+    dilated_weight_grad = dilated_sum.transpose(1, 0).reshape(3, 3, local_mid, -1)
+    expand_bias_grad, expand_gain_grad = sums3[0], sums3[1]
+    dilated_bias_grad, dilated_gain_grad = sums2[0], sums2[1]
+    reduce_bias_grad, reduce_gain_grad = sums1[0], sums1[1]
+
+    return (
+        predictions,
+        features_grad,
+        reduce_weight_grad,
+        reduce_gain_grad,
+        reduce_bias_grad,
+        dilated_weight_grad,
+        dilated_gain_grad,
+        dilated_bias_grad,
+        expand_weight_grad,
+        expand_gain_grad,
+        expand_bias_grad,
+        aspp_weight_grad,
+        aspp_gain_grad,
+        aspp_bias_grad,
+        task_weight_grad,
+    )
+
+
 def solution(mesh):
     placed = (
         P("pix", None, "ch"),
@@ -341,7 +1715,7 @@
         P("pix", None, None),
     )
     return jax.shard_map(
-        on_device,
+        fast_device if (mesh.shape["pix"], mesh.shape["ch"]) == (PHASES, 4) else on_device,
         mesh=mesh,
         in_specs=placed,
         out_specs=(

time: 1860 us -> 422 us (0.23)
  waiting for transfers between devices: 1060 us -> 0 us
  Pallas kernels: 0 us -> 384 us
  blocking collectives: 375 us -> 0 us
  matrix products: 164 us -> 0.25 us
  starting transfers between devices: 93.6 us -> 0 us
  other arithmetic: 66.4 us -> 4.68 us
  local copies, waits for them, and re-layouts: 70 us -> 25.1 us
  between operations: 26.1 us -> 1.34 us
    unnamed x13 -> x0, waiting for transfers between devices: 649 us -> none
    pallas_call x0 -> x6, Pallas kernels: none -> 384 us  [the longest x1 211 us: run_backward(): pl.pallas_call(backward, out_shape=outs, in_specs=specs, out_specs=[vmem,...]
    psum x14 -> x0, blocking collectives: 375 us -> none  [the longest x4 118 us: norm_grad(): lax.psum((jnp.sum(grad_out, axis=axes, keepdims=True), jnp.sum(grad_out *...]
    reduce_scatter x5 -> x0, waiting for transfers between devices: 170 us -> none  [the longest x1 66.8 us: on_device(): lax.psum_scatter(reduce_weight_local, 'pix', scatter_dimension=0, tiled=T...]
    dot_general x119 -> x1, matrix products: 164 us -> 0.25 us  [fast_device(): jnp.einsum('po,pq->oq', target_here[:, :32], target_here[:, :32], precisi...]
    ppermute x24 -> x0, waiting for transfers between devices: 154 us -> none  [the longest x20 147 us: from_behind(): lax.ppermute(value, axis, [(source, source + steps) for source in range(f...]
    ppermute x24 -> x0, starting transfers between devices: 92.8 us -> none  [the longest x20 81.8 us: from_behind(): lax.ppermute(value, axis, [(source, source + steps) for source in range(f...]
    all_gather x4 -> x0, waiting for transfers between devices: 82.8 us -> none  [gather_channels(): return lax.all_gather(value, 'ch', axis=1, tiled=True)]
  transfers between devices with their start and end apart: 35 -> 0, of which waited for: 17 -> 0; matrix products, arithmetic and copies ran while one was open for 8% -> 0% of each run, Pallas kernels for 0% -> 0%
where the time goes in v1:
time: 422 us; the launch traced here: 415 us
  Pallas kernels  384 us (91%)
  local copies, waits for them, and re-layouts  25.1 us (6%)
  other arithmetic  4.68 us (1%)
    pallas_call x1, Pallas kernels, run_backward(): pl.pallas_call(backward, out_shape=outs, in_specs=specs, out_specs=[vmem,...  211 us
    pallas_call x3, Pallas kernels, call(): pl.pallas_call(kernel, out_shape=outs, in_specs=[vmem] * len(arrays), out...  103 us
    pallas_call x1, Pallas kernels, run_pyramid(): pl.pallas_call(pyramid, out_shape=outs, in_specs=specs, out_specs=[vmem]...  52.8 us
    pallas_call x1, Pallas kernels, run_finish(): pl.pallas_call(finish_pyramid, grid=(steps,), out_shape=shape((steps, n,...  17.1 us
    unnamed x24, local copies, waits for them, and re-layouts  11 us

profile of v1, /device:TPU:0, one launch (start us, length us, event | category | flops | bytes accessed | tf_op | source)
XLA Modules:
  0.0 415.5 jit_solution(111254983691182445)
XLA Ops:
  0.6 0.7 convert_element_type.8
  1.3 0.1 reshape_reshape.9
  1.5 0.1 copy.50
  1.6 0.1 broadcast_in_dim.40
  1.7 1.0 broadcast_in_dim.41.valid
  2.7 0.1 pad.22.clone
  2.8 1.4 maximum_maximum_fusion.2
  4.1 0.7 convert_bitcast_fusion
  4.9 0.1 reshape.115
  5.0 0.8 reshape.101
  5.7 0.8 reshape.102
  6.5 0.2 concatenate.23
  6.7 0.6 pad.9.heads
  7.3 0.1 mul.18
  7.4 0.2 slice.54
  7.6 1.1 copy.52
  8.7 0.1 copy.53
  8.7 0.2 broadcast_multiply_fusion
  9.0 0.1 pad.18.clone
  9.0 1.0 pad_maximum_fusion.targets
  10.0 0.5 copy.55
  10.5 0.3 reshape_reshape.11
  10.8 0.2 fusion
  11.1 0.6 pad.10.square
  11.7 0.0 copy-start.6
  11.7 0.0 copy-start.7
  11.7 38.0 %stage_one.1 = (bf16[1024,512]{1,0:T(8,128)(2,1)}, bf16[512,512]{1,0:T(8,128)(2,1)}, bf16[512,512]{1,0:T(8,128)(2,1)}, f32[4,40,256]{2,1,0:T(8,128)}, f32[8,128,...) custom-call(bf16[1024,512]{1,0:T(8,128)(2,1)} %bitcast.65, ...), custom_call_target="tpu_custom_call" | custom-call | tf_op jit(solution)/shard_map/stage_one/pallas_call | solution.py:341
  49.7 0.0 copy-start.1
  49.8 27.8 %stage_two.1 = (f32[1024,128]{1,0:T(8,128)}, bf16[1024,512]{1,0:T(8,128)(2,1)}, bf16[1024,1152]{1,0:T(8,128)(2,1)}, f32[8,128]{1,0:T(8,128)}) custom-call(bf16[8,6,32,128]{3,2,1,0:T(8,128)(2,1)} %get-tuple-element.44.padded, f32[1024,128]{1,0:T(8,128)} %broadcast_in_dim.41.valid, bf16[1152,512]{1,0:T(8,128)(2,1)} %bitcast.57, ...), custom_call_target="tpu_custom_call" | custom-call | tf_op jit(solution)/shard_map/stage_two/pallas_call | solution.py:341
  77.6 0.0 copy-done.6
  77.6 0.0 copy-done.7
  77.6 0.7 maximum_maximum_fusion.affine.affine3
  78.3 37.1 %stage_three.1 = (f32[1024,512]{1,0:T(8,128)}, bf16[1024,512]{1,0:T(8,128)(2,1)}, f32[8,512]{1,0:T(8,128)}) custom-call(bf16[1024,512]{1,0:T(8,128)(2,1)} %get-tuple-element.45.full.full2, bf16[512,512]{1,0:T(8,128)(2,1)} %get-tuple-element.46.weight.expand, bf16[1024,512]{1,0:T(8,128)(2,1)} %get-tuple-element.47.masked, ...), custom_call_target="tpu_custom_call" | custom-call | tf_op jit(solution)/shard_map/stage_three/pallas_call | solution.py:341
  115.4 0.0 copy-done.1
  115.4 0.1 reshape.105
  115.6 0.7 slice.57.affine
  116.4 0.1 copy.57
  116.5 0.8 slice.59.heads
  117.3 52.8 %pyramid.1 = (bf16[1024,768]{1,0:T(8,128)(2,1)}, f32[8,32,128]{2,1,0:T(8,128)}, f32[32,768]{1,0:T(8,128)}, f32[8,256]{1,0:T(8,128)}, bf16[1024,512]{1,0:T(8,128)(2,1)}) custom-call(bf16[1024,512]{1,0:T(8,128)(2,1)} %get-tuple-element.48.trunk, bf16[3,3,3,512,256]{4,3,2,1,0:T(8,128)(2,1)} %weight.5, f32[8,768]{1,0:T(8,128)} %slice.57.affine, ...), custom_call_target="tpu_custom_call" | custom-call | tf_op jit(solution)/shard_map/pyramid/pallas_call | solution.py:1096
  170.1 1.2 reshape.107
  171.2 0.3 copy.58
  171.5 0.8 copy.60
  172.3 211.4 %backward.1 = (bf16[1024,512]{1,0:T(8,128)(2,1)}, bf16[4,27,32,512]{3,2,1,0:T(8,128)(2,1)}, f32[64,1152]{1,0:T(8,128)}, f32[128,256]{1,0:T(8,128)}, f32[256,128]...) custom-call(bf16[1024,768]{1,0:T(8,128)(2,1)} %get-tuple-element.53.grads, ...), custom_call_target="tpu_custom_call" | custom-call | tf_op jit(solution)/shard_map/backward/pallas_call | solution.py:1542
  383.7 1.3 slice_bitcast_fusion
  385.0 1.1 reshape.110
  386.1 0.7 copy.61
  386.8 1.4 fusion.3
  388.2 17.1 %finish_pyramid.1 = f32[27,512,32]{2,1,0:T(8,128)} custom-call(bf16[4,27,32,512]{3,2,1,0:T(8,128)(2,1)} %get-tuple-element.70.parts), custom_call_target="tpu_custom_call" | custom-call | tf_op jit(solution)/shard_map/finish_pyramid/pallas_call | solution.py:1564
  405.3 0.0 copy-start.5
  405.3 0.0 copy-start.4
  405.3 0.0 copy-start
  405.3 6.0 %copy.62 = f32[3,3,3,512,32]{3,4,2,1,0:T(8,128)} copy(f32[3,3,3,512,32]{4,3,2,1,0:T(8,128)} %bitcast.56) | data formatting | bytes 3538944
  411.3 0.0 copy-start.3
  411.3 0.0 copy-done.5
  411.3 0.7 dynamic-slice_bitcast_fusion
  411.9 0.0 copy-done.4
  411.9 0.1 reshape.113
  412.1 0.6 slice.74
  412.8 0.0 copy-done
  412.8 1.0 copy.69
  413.7 0.0 copy-done.3
  413.7 0.7 copy.70
  414.4 0.0 copy-done.2
  414.4 0.7 copy.71
  (13 shorter events, 0.2 us)
Async XLA Ops:
  11.7 65.9 %copy-start.6 = (f32[512]{0:T(512)S(1)}, f32[512]{0:T(512)}, u32[]{:S(2)}) copy-start(f32[512]{0:T(512)} %param.26) | copy-start | bytes 6148
  11.7 65.9 %copy-start.7 = (f32[512]{0:T(512)S(1)}, f32[512]{0:T(512)}, u32[]{:S(2)}) copy-start(f32[512]{0:T(512)} %param.25) | copy-start | bytes 6148
  49.7 65.6 %copy-start.1 = (f32[4,40,256]{2,1,0:T(8,128)S(1)}, f32[4,40,256]{2,1,0:T(8,128)}, u32[]{:S(2)}) copy-start(f32[4,40,256]{2,1,0:T(8,128)} %get-tuple-element.49) | copy-start | bytes 491524
  405.3 6.0 %copy-start.5 = (f32[8,256]{1,0:T(8,128)S(1)}, f32[8,256]{1,0:T(8,128)}, u32[]{:S(2)}) copy-start(f32[8,256]{1,0:T(8,128)} %get-tuple-element.71) | copy-start | bytes 24580
  405.3 6.7 %copy-start.4 = (f32[32,768]{1,0:T(8,128)S(1)}, f32[32,768]{1,0:T(8,128)}, u32[]{:S(2)}) copy-start(f32[32,768]{1,0:T(8,128)} %get-tuple-element.72) | copy-start | bytes 294916
  405.3 7.5 %copy-start = (bf16[1024,512]{1,0:T(8,128)(2,1)S(1)}, bf16[1024,512]{1,0:T(8,128)(2,1)}, u32[]{:S(2)}) copy-start(bf16[1024,512]{1,0:T(8,128)(2,1)} %get-tuple-element.63) | copy-start | bytes 3145732
  411.3 2.5 copy-start.3
  411.3 3.1 copy-start.2

commit v2 on v1

--- a/solution.py
+++ b/solution.py
@@ -336,13 +336,13 @@
     return jax.ShapeDtypeStruct(dims, dtype)
 
 
-def call(name, cid, kernel, arrays, outs, scratch):
-    vmem = pl.BlockSpec(memory_space=pltpu.VMEM)
+def call(name, cid, kernel, arrays, outs, scratch, hbm_ins=(), hbm_outs=()):
+    vmem, hbm = pl.BlockSpec(memory_space=pltpu.VMEM), pl.BlockSpec(memory_space=pl.ANY)
     return pl.pallas_call(
         kernel,
         out_shape=outs,
-        in_specs=[vmem] * len(arrays),
-        out_specs=[vmem] * len(outs),
+        in_specs=[hbm if i in hbm_ins else vmem for i in range(len(arrays))],
+        out_specs=[hbm if i in hbm_outs else vmem for i in range(len(outs))],
         scratch_shapes=scratch,
         compiler_params=pltpu.CompilerParams(
             collective_id=cid, has_side_effects=True, vmem_limit_bytes=VMEM_BYTES
@@ -516,7 +516,7 @@
     return x / (1.0 + jnp.exp(-x))
 
 
-def gather_over_ch(full, n, tile, tiles, near_sems, far_sems, hop_sems, ready):
+def gather_over_ch(full, n, tile, tiles, near_sems, far_sems, hop_sems, ready, between=None):
     p, c = lax.axis_index("pix"), lax.axis_index("ch")
 
     def part(owner, t):
@@ -528,6 +528,8 @@
         src = part(c, t)
         far.append(push(src, src, far_sems.at[0, t], far_sems.at[1, t], (p, c ^ 2)))
         near.append(push(src, src, near_sems.at[0, t], near_sems.at[1, t], (p, c ^ 1)))
+    if between is not None:
+        between()
     for t in range(tiles):
         far[t].wait_recv()
         src = part(c ^ 2, t)
@@ -755,16 +757,19 @@
 
 
 def stage_three(full, weight, masked, valid, affine, *refs):
-    (norm, classes, stat) = refs[:3]
-    (hidden, trunk, send, recv, stat_sems, class_sems, own_sem) = refs[3:]
+    (norm, classes, stat, inputs) = refs[:4]
+    (hidden, trunk, send, recv, stat_sems, class_sems, own_sem, in_sems) = refs[4:]
     p, c = lax.axis_index("pix"), lax.axis_index("ch")
     pixels, n = masked.shape
-    barrier, expected = greet((), FAR_FIRST)
+    barrier, expected = greet((1, 2), FAR_FIRST)
     tile = pixels // TILES
     for t in range(TILES):
         at = pl.ds(t * tile, tile)
         hidden[at] = jnp.dot(full[at], weight[...], preferred_element_type=f32)
     pl.semaphore_wait(barrier, expected)
+    far = push(masked, inputs.at[c], in_sems.at[0, 0], in_sems.at[1, 0], (p, c ^ 2))
+    near = push(masked, inputs.at[c], in_sems.at[0, 1], in_sems.at[1, 1], (p, c ^ 1))
+    mine = keep(masked, inputs.at[c], own_sem.at[1])
     center, scale, count = norm_stats(hidden, valid, pixels, send, recv, stat_sems)
     stat[0:1] = center
     stat[1:2] = scale
@@ -797,19 +802,30 @@
         )
     finish(p)
     copies.append(keep(trunk.at[rows(p * 128, 128)], classes.at[rows(p * 128, 128)], own_sem.at[0]))
+    far.wait_recv()
+    hop = push(inputs.at[c ^ 2], inputs.at[c ^ 2], in_sems.at[0, 2], in_sems.at[1, 2], (p, c ^ 1))
+    far.wait_send()
+    near.wait()
+    mine.wait()
+    hop.wait()
     for copy in copies:
         copy.wait()
 
 
 def run_stage_three(cid, full, weight, masked, valid, affine):
     pixels, n = masked.shape
-    outs = [shape((pixels, n), f32), shape((pixels, n), bf16), shape((8, n), f32)]
+    outs = [
+        shape((pixels, n), f32),
+        shape((pixels, n), bf16),
+        shape((8, n), f32),
+        shape((SPLIT, pixels, n), bf16),
+    ]
     scratch = (
         [pltpu.VMEM((pixels, n), f32), pltpu.VMEM((pixels, n), bf16)]
         + stat_scratch(n)
-        + [dma(2, PHASES), dma(1)]
-    )
-    return call("stage_three", cid, stage_three, [full, weight, masked, valid, affine], outs, scratch)
+        + [dma(2, PHASES), dma(2), dma(2, 3)]
+    )
+    return call("stage_three", cid, stage_three, [full, weight, masked, valid, affine], outs, scratch, hbm_outs=(3,))
 
 
 RATE_ROWS = tuple(rate // ROW_CLASSES for rate in aspp_rates)
@@ -879,12 +895,12 @@
 
 
 def pyramid(trunk, weight, affine, heads, targets, square, *refs):
-    (full, predictions, head_grad, sums, other) = refs[:5]
-    refs = refs[1:]
+    (full, predictions, head_grad, sums, others, picks) = refs[:6]
+    refs = refs[2:]
     (wide, sides, own, out, near, cross, hidden, pre, grad, branch) = refs[4:14]
     (s_send, s_ch, s_mid, s_pix, b_send, b_ch, b_mid, b_pix) = refs[14:22]
     (h_send, h_ch, h_mid, h_pix, h_sum, p_send, p_ch) = refs[22:29]
-    (w_sems, near_sems, far_sems, ch_sems, pix_sems, g_near, g_far, g_hop, y_sems) = refs[29:]
+    (w_sems, near_sems, far_sems, ch_sems, pix_sems, g_near, g_far, g_hop, y_sems, picked, pick_sems) = refs[29:]
     p, c = lax.axis_index("pix"), lax.axis_index("ch")
     k, x = lax.rem(c, 2), c // 2
     m = weight.shape[4]
@@ -901,7 +917,14 @@
     target, mask = targets[mine, :32], targets[mine, 32:33]
     grad[...] = jnp.dot(target, scaled, precision=highest) * mask
     pl.semaphore_wait(barrier, expected)
-    to_other = push(trunk, other, y_sems.at[0], y_sems.at[1], (p ^ 1, c))
+    halves = [pl.ds(0, trunk.shape[0] // 2), pl.ds(trunk.shape[0] // 2, trunk.shape[0] // 2)]
+    to_y, to_z = [None, None], [None, None]
+    for i in range(2):
+        to_y[i] = push(trunk.at[halves[i]], others.at[0, halves[i]], y_sems.at[0, i], y_sems.at[1, i], (p ^ 1, c))
+        h = 1 - i
+        to_z[h] = push(
+            trunk.at[halves[h]], others.at[1, halves[h]], y_sems.at[0, 2 + i], y_sems.at[1, 2 + i], (p ^ 2, c)
+        )
 
     copies = []
     for j in range(3):
@@ -930,6 +953,11 @@
                 for h in range(2)
             ]
         )
+        if j == 1:
+            to_y[0].wait_recv()
+            on_z = push(others.at[0, halves[0]], others.at[2, halves[0]], y_sems.at[0, 4], y_sems.at[1, 4], (p ^ 2, c))
+            to_z[1].wait_recv()
+            on_y = push(others.at[1, halves[1]], others.at[2, halves[1]], y_sems.at[0, 5], y_sems.at[1, 5], (p ^ 1, c))
         if j > 0:
             copies[j - 1] = cross_chips(copies[j - 1], j - 1, own, near, cross, far_sems)
     copies[2] = cross_chips(copies[2], 2, own, near, cross, far_sems)
@@ -1023,6 +1051,17 @@
         full[mine, at] = (affine[0:1, at] * scale[j : j + 1] * value).astype(bf16)
     far = push(full.at[mine], full.at[mine], g_far.at[0], g_far.at[1], (p, c ^ 2))
     by = push(full.at[mine], full.at[mine], g_near.at[0], g_near.at[1], (p, c ^ 1))
+    group = lax.rem(p, 4)
+    pick = pick_rows(m, m, 0)
+    for j in range(3):
+        value = lax.dot_general(
+            pick, full[mine, j * m : (j + 1) * m], contract1, preferred_element_type=f32
+        ).astype(bf16)
+        for g in range(4):
+            picked[g, j * 64 : (j + 1) * 64] = value[g * 64 : (g + 1) * 64]
+    sent_picks = [
+        push(picked.at[group ^ i], picks.at[i - 1], pick_sems.at[0, i], pick_sems.at[1, i], (p ^ i, c)) for i in (3, 1, 2)
+    ]
     for copy in background:
         copy.wait()
     own_rows = add_up(h_pix, PHASES)
@@ -1040,7 +1079,17 @@
     hop.wait()
     for copy in last:
         copy.wait()
-    to_other.wait()
+    to_y[0].wait_send()
+    to_z[1].wait_send()
+    for copy in [to_y[1], to_z[0], on_y, on_z] + sent_picks:
+        copy.wait()
+
+
+def pick_rows(m, count, first):
+    row = lax.broadcasted_iota(jnp.int32, (count, m), 0)
+    col = lax.broadcasted_iota(jnp.int32, (count, m), 1)
+    source = (4 * (row % 64 // 32) + row // 64 + first) * 32 + row % 32
+    return jnp.where(col == source, 1.0, 0.0).astype(bf16)
 
 
 def cross_chips(near_copies, j, own, near, cross, sems):
@@ -1061,7 +1110,8 @@
         shape((PHASES, 32, 128), f32),
         shape((32, 3 * m), f32),
         shape((8, m), f32),
-        shape((pixels, n), bf16),
+        shape((3, pixels, n), bf16),
+        shape((3, 192, quarter), bf16),
     ]
     small = [pltpu.VMEM((8, m), f32), pltpu.VMEM((SPLIT, 8, m), f32), pltpu.VMEM((8, m), f32), pltpu.VMEM((PHASES, 8, m), f32)]
     scratch = (
@@ -1088,7 +1138,8 @@
             pltpu.VMEM((32, quarter), f32),
             pltpu.VMEM((SPLIT, 32, quarter), f32),
         ]
-        + [dma(9, 3), dma(2, 3, 2), dma(2, 3), dma(5, 2, SPLIT), dma(4, 2, PHASES), dma(2), dma(2), dma(2), dma(2)]
+        + [dma(9, 3), dma(2, 3, 2), dma(2, 3), dma(5, 2, SPLIT), dma(4, 2, PHASES), dma(2), dma(2), dma(2), dma(2, 6)]
+        + [pltpu.VMEM((4, 192, quarter), bf16), dma(2, 4)]
     )
     vmem = pl.BlockSpec(memory_space=pltpu.VMEM)
     specs = [vmem] * 6
@@ -1097,13 +1148,16 @@
         pyramid,
         out_shape=outs,
         in_specs=specs,
-        out_specs=[vmem] * len(outs),
+        out_specs=[vmem] * 4 + [pl.BlockSpec(memory_space=pl.ANY), vmem],
         scratch_shapes=scratch,
         compiler_params=pltpu.CompilerParams(
             collective_id=cid, has_side_effects=True, vmem_limit_bytes=VMEM_BYTES
         ),
         name="pyramid",
     )(trunk, weight, affine, heads, targets, square)
+
+
+PACE = (2, 10, 16, 18)
 
 
 def packed_sums(values, send):
@@ -1133,16 +1187,16 @@
 
 
 def backward(
-    grads, trunk, other, weight, norm3, masked, valid, expand, affine3, norm2, affine2, full2, taps, dilated,
-    norm1, affine1, reduce_rows, stats1, stats2, stats3, *refs
+    grads, trunk, others, weight, norm3, masked, valid, expand, affine3, norm2, affine2, full2, taps, dilated,
+    norm1, affine1, reduce_rows, stats1, stats2, stats3, picks, inputs, *refs
 ):
     outs, scratch = refs[:8], refs[8:]
     (features_grad, aspp_parts, dilated_grad, expand_grad, reduce_grad, sums3_out, sums2_out, sums1_out) = outs
-    (wide, moved, acc, dsend, drecv, tpad, picked, picked_in, turned, zsend, zown) = scratch[:11]
+    (wide, moved, acc, dsend, drecv, tpad, r_in, picked_in, turned, zsend, r_y) = scratch[:11]
     (gp3, g3, own, out, near, cross, hidden, gp2, g2, prod, edges, g1) = scratch[11:23]
     gp1, lanes = gp2, own
-    (st3, st3r, st2, st2r, st1, st1r, e_part, e_mid, e_sum, d_part, d_sum, r_part, r_mid, r_sum) = scratch[23:37]
-    (w_sems, d_sems, y_sems, z_sems, near_sems, far_sems, st_sems, gn, gf, gh, gn1, gf1, gh1, edge_sems, ch_sems, pix_sems, own_sems) = scratch[37:]
+    (st3, st3r, st2, st2r, st1, st1r, e_part, e_mid, e_in, e_y, e_sum, d_part, d_in, d_y, d_sum, r_mid, r_sum) = scratch[23:40]
+    (w_sems, d_sems, y_sems, z_sems, near_sems, far_sems, st_sems, gn, gf, gh, gn1, gf1, gh1, edge_sems, ch_sems, pix_sems, pair_sems, own_sems, tap_sems, in_sems) = scratch[40:]
     p, c = lax.axis_index("pix"), lax.axis_index("ch")
     y, z = lax.rem(p, 2), p // 2
     pixels, n = norm3.shape
@@ -1155,16 +1209,19 @@
     barrier, expected = greet((1, 2, 3), FAR_FIRST)
     loads = load_pyramid(weight, wide, w_sems)
 
-    row = lax.broadcasted_iota(jnp.int32, (m, m), 0)
-    col = lax.broadcasted_iota(jnp.int32, (m, m), 1)
-    source = (2 * ((col % 128) // 32) + col // 128) * 32 + col % 32
-    pick = jnp.where(row == source, 1.0, 0.0).astype(bf16)
-    for j in range(3):
-        value = jnp.dot(grads[:, j * m : (j + 1) * m], pick, preferred_element_type=f32).astype(bf16)
-        picked[0, j] = value[:, :128]
-        picked[1, j] = value[:, 128:]
+    group, upper = lax.rem(p, 4), p // 4
+    quarter = picks.shape[2]
     pl.semaphore_wait(barrier, expected)
-    sent_picks = push(picked.at[1 - y], picked_in, y_sems.at[0], y_sems.at[1], (p ^ 1, c))
+    mine = rows(c * quarter, quarter)
+    sent_picks = [
+        push(picks, picked_in.at[:, :, mine], y_sems.at[0, k], y_sems.at[1, k], (p, c ^ k)) for k in (2, 3, 1)
+    ] + [keep(picks, picked_in.at[:, :, mine], y_sems.at[0, 0])]
+    filled = [keep(trunk, tpad.at[0, 64 : 64 + pixels], y_sems.at[2, 0])] + [
+        keep(others.at[k - 1], tpad.at[k, 64 : 64 + pixels], y_sems.at[2, k]) for k in (1, 2, 3)
+    ]
+    for i in range(4):
+        tpad[i, :64] = jnp.zeros((64, n), bf16)
+        tpad[i, 64 + pixels :] = jnp.zeros((64, n), bf16)
 
     for j in range(3):
         q = RATE_COLS[j]
@@ -1206,10 +1263,16 @@
             )
         back.append(keep(dsend.at[h, rows(p * 128, 128)], drecv.at[h, rows(p * 128, 128)], own_sems.at[h]))
 
-    for i, source in enumerate((trunk, other)):
-        tpad[i, :64] = jnp.zeros((64, n), bf16)
-        tpad[i, 64 : 64 + pixels] = source[...]
-        tpad[i, 64 + pixels :] = jnp.zeros((64, n), bf16)
+    all_inputs = [
+        keep(inputs.at[i // 2, pl.ds(i % 2 * n, n)], wide.at[i, :, :n], in_sems.at[i]) for i in range(8)
+    ]
+    cut = moved.shape[2]
+    own_taps = [
+        keep(taps.at[:, :cut], moved.at[0], tap_sems.at[0]),
+        keep(taps.at[:, cut:], moved.at[1, :, : taps.shape[1] - cut], tap_sems.at[1]),
+    ]
+
+    place = lax.broadcasted_iota(jnp.int32, (64, pixels), 1) % 32
 
     def turn(i, part):
         at = slice(i * pixels, (i + 1) * pixels)
@@ -1217,12 +1280,23 @@
             q = RATE_COLS[j]
             plain = part(j)
             value = plain.astype(f32)
-            for b, piece in enumerate((move_cols(value, -q).astype(bf16), plain, move_cols(value, q).astype(bf16))):
-                turned[j, b * 128 : (b + 1) * 128, at] = piece.T
-
-    turn(0, lambda j: picked[y, j])
-    sent_picks.wait()
-    turn(1, lambda j: picked_in[j])
+            turned[j, :64, at] = jnp.where(place >= 32 - q, 0.0, pltpu.roll(value, pixels - q, 1)).astype(bf16)
+            turned[j, 64:128, at] = plain
+            turned[j, 128:, at] = jnp.where(place < q, 0.0, pltpu.roll(value, q, 1)).astype(bf16)
+
+    pick = pick_rows(m, 64, group)
+    turn(
+        0,
+        lambda j: lax.dot_general(
+            pick, grads[:, j * m : (j + 1) * m], contract1, preferred_element_type=f32
+        ).astype(bf16),
+    )
+    for copy in sent_picks:
+        copy.wait()
+    for k in (1, 2, 3):
+        turn(k, lambda j: picked_in[k - 1, j * 64 : (j + 1) * 64])
+    for copy in filled:
+        copy.wait()
     for j in range(3):
         s = RATE_ROWS[j] * 32
         for a in range(3):
@@ -1234,7 +1308,7 @@
             else:
                 low, high, start = 0, -(-(pixels - s) // 128) * 128, 64 + s
             value = None
-            for i in range(2):
+            for i in range(4):
                 term = jnp.dot(
                     turned[j, :, i * pixels + low : i * pixels + high],
                     tpad[i, start : start + high - low],
@@ -1243,15 +1317,25 @@
                 value = term if value is None else value + term
             value = value.astype(bf16)
             for b in range(3):
-                for to in range(4):
-                    at = b * 128 + to * 32
+                for to in range(2):
+                    at = b * 64 + to * 32
                     zsend[to, (3 * j + a) * 3 + b] = value[at : at + 32]
     for copy in back:
         copy.wait()
-    zcopies = [
-        push(zsend.at[z ^ k], aspp_parts.at[z], z_sems.at[0, k], z_sems.at[1, k], (p ^ (2 * k), c)) for k in (3, 2, 1)
-    ]
-    zcopies.append(keep(zsend.at[z], aspp_parts.at[z], own_sems.at[2]))
+    zcopies = [keep(zsend.at[upper], aspp_parts.at[0], own_sems.at[2])]
+
+    def send_parts(first, end):
+        for i in range(first, end):
+            zcopies.append(
+                push(zsend.at[1 - upper, i], aspp_parts.at[1, i], z_sems.at[0, i], z_sems.at[1, i], (p ^ 4, c))
+            )
+
+    send_parts(0, PACE[0])
+
+    def over_z(blocks, sums, sems, own_sem):
+        return [
+            push(blocks.at[z ^ k], sums.at[z], sems.at[0, k], sems.at[1, k], (p ^ (2 * k), c)) for k in (3, 2, 1)
+        ] + [keep(blocks.at[z], sums.at[z], own_sem)]
 
     def norm_back(grad, norm, sums, scale, gain, v):
         return gain * scale * (grad - v * (sums[0] + norm * sums[1]) / count)
@@ -1269,6 +1353,7 @@
     bias, gain = loop(pixels // 32, three, (zero, zero))
     packed_sums((total(bias), total(gain)), st3)
     pix_exchange(st3, st3r, st_sems.at[0])
+    send_parts(PACE[0], PACE[1])
     sums = unpacked_sums(st3r, n // 128, 2)
     sums3_out[0:1] = sums[0]
     sums3_out[1:2] = sums[1]
@@ -1306,6 +1391,12 @@
     bias, gain = loop(pixels // 128, two, (bias, gain))
     packed_sums((total(bias), total(gain)), st2)
     pix_exchange(st2, st2r, st_sems.at[1])
+    send_parts(PACE[1], PACE[2])
+    for copy in e_copies:
+        copy.wait()
+    e_to_y = push(
+        e_mid.at[:, :, rows((1 - y) * 256, 256)], e_in, pair_sems.at[0, 0], pair_sems.at[1, 0], (p ^ 1, c)
+    )
     sums2 = unpacked_sums(st2r, 1, 2)
     sums2_out[0:1] = sums2[0]
     sums2_out[1:2] = sums2[1]
@@ -1320,16 +1411,18 @@
         loop(tile // 128, step, 0)
 
     gather_over_ch(g2, mid, tile, TILES, gn, gf, gh, ready2)
-    for t in range(TILES):
-        at = pl.ds(t * tile, tile)
-        prod[at] = lax.dot_general(g2[at], dilated[...], contract1, preferred_element_type=f32)
+
+    e_to_y.wait()
+    for d in range(4):
+        e_y[d] = (e_mid[d, :, rows(y * 256, 256)].astype(f32) + e_in[d].astype(f32)).astype(bf16)
+    pix_copies = over_z(e_y, e_sum, pix_sems.at[0], own_sems.at[5])
 
     place = lax.broadcasted_iota(jnp.int32, (128, mid), 0) % 32
 
     def across(i, a):
         beta = i % COL_CLASSES
-        two_on = (i - beta + (beta + 2) % 4) * 128
-        here = slice(i * 128, (i + 1) * 128)
+        two_on = (beta + 2) % 4 * 128
+        here = slice(beta * 128, (beta + 1) * 128)
         there = slice(two_on, two_on + 128)
         lane = lambda b: slice((3 * a + b) * mid, (3 * a + b + 1) * mid)
         left, right = prod[there, lane(0)], prod[there, lane(2)]
@@ -1341,6 +1434,10 @@
 
     for i in range(PHASES):
         at = slice(i * 128, (i + 1) * 128)
+        if i % COL_CLASSES == 0:
+            prod[...] = lax.dot_general(
+                g2[i * 128 : (i + COL_CLASSES) * 128], dilated[...], contract1, preferred_element_type=f32
+            )
         up, same, down = across(i, 0), across(i, 1), across(i, 2)
         zero = jnp.zeros((32, mid), f32)
         hidden[at] = same + jnp.concatenate([up[32:], zero]) + jnp.concatenate([zero, down[:96]])
@@ -1372,10 +1469,21 @@
     def _():
         edges[3] = jnp.zeros((PHASES, 32, mid), bf16)
 
-    value = lax.dot_general(g2[...], taps[...], contract0, preferred_element_type=f32).astype(bf16)
+    for copy in own_taps:
+        copy.wait()
+    value = jnp.concatenate(
+        [
+            lax.dot_general(g2[...], moved[0], contract0, preferred_element_type=f32).astype(bf16),
+            lax.dot_general(
+                g2[...], moved[1, :, : taps.shape[1] - cut], contract0, preferred_element_type=f32
+            ).astype(bf16),
+        ],
+        axis=1,
+    )
     out_rows = SPLIT * mid // PHASES
     for d in range(PHASES):
-        d_part[d] = value[d * out_rows : (d + 1) * out_rows]
+        d_part[d % 2, d // 2] = value[d * out_rows : (d + 1) * out_rows]
+    d_to_y = push(d_part.at[1 - y], d_in, pair_sems.at[0, 1], pair_sems.at[1, 1], (p ^ 1, c))
 
     @pl.when(jnp.logical_not(last))
     def _():
@@ -1386,6 +1494,8 @@
     def _():
         to_last().wait_send()
         to_next().wait_recv()
+
+    send_parts(PACE[2], PACE[3])
 
     bias, gain = jnp.zeros((8, mid), f32), jnp.zeros((8, mid), f32)
     for i in range(PHASES):
@@ -1398,6 +1508,7 @@
         bias, gain = bias + fold(grad), gain + fold(grad * norm)
     packed_sums((total(bias), total(gain)), st1)
     pix_exchange(st1, st1r, st_sems.at[2])
+    send_parts(PACE[3], 27)
     sums1 = unpacked_sums(st1r, 1, 2)
     sums1_out[0:1] = sums1[0]
     sums1_out[1:2] = sums1[1]
@@ -1411,36 +1522,27 @@
 
         loop(tile // 128, step, 0)
 
-    gather_over_ch(g1, mid, tile, TILES, gn1, gf1, gh1, ready1)
-    value = lax.dot_general(masked[...], g1[...], contract0, preferred_element_type=f32).astype(bf16)
-    for d in range(SPLIT):
-        r_part[d] = value[:, d * mid : (d + 1) * mid]
-    r_copies = [
-        push(r_part.at[c ^ k], r_mid.at[rows(c * n, n)], ch_sems.at[1, 0, k], ch_sems.at[1, 1, k], (p, c ^ k))
-        for k in (2, 3, 1)
-    ]
-    r_copies.append(keep(r_part.at[c], r_mid.at[rows(c * n, n)], own_sems.at[4]))
-    for copy in e_copies:
-        copy.wait()
-
-    def wanted(to):
-        return e_mid.at[to // 2, :, rows(lax.rem(to, 2) * 256, 256)]
-
-    pix_copies = [
-        push(wanted(p ^ k), e_sum.at[p], pix_sems.at[0, 0, k], pix_sems.at[0, 1, k], (p ^ k, c)) for k in FAR_FIRST
-    ]
-    pix_copies.append(keep(wanted(p), e_sum.at[p], own_sems.at[5]))
-    pix_copies += [
-        push(d_part.at[p ^ k], d_sum.at[p], pix_sems.at[1, 0, k], pix_sems.at[1, 1, k], (p ^ k, c)) for k in FAR_FIRST
-    ]
-    pix_copies.append(keep(d_part.at[p], d_sum.at[p], own_sems.at[6]))
-    for copy in r_copies:
-        copy.wait()
-    pix_copies += [
-        push(r_mid.at[rows((p ^ k) * 256, 256)], r_sum.at[p], pix_sems.at[2, 0, k], pix_sems.at[2, 1, k], (p ^ k, c))
-        for k in FAR_FIRST
-    ]
-    pix_copies.append(keep(r_mid.at[rows(p * 256, 256)], r_sum.at[p], own_sems.at[7]))
+    late = []
+
+    def between():
+        for copy in all_inputs:
+            copy.wait()
+        own_g1 = g1[:, rows(c * mid, mid)]
+        for i in range(SPLIT):
+            value = lax.dot_general(wide[2 * i, :, :n], own_g1[:n], contract0, preferred_element_type=f32)
+            value = value + lax.dot_general(wide[2 * i + 1, :, :n], own_g1[n:], contract0, preferred_element_type=f32)
+            r_mid[i] = value.astype(bf16).reshape(2, 256, mid)
+        late.append(push(r_mid.at[:, 1 - y], r_in, pair_sems.at[0, 2], pair_sems.at[1, 2], (p ^ 1, c)))
+        d_to_y.wait()
+        for d in range(4):
+            d_y[d] = (d_part[y, d].astype(f32) + d_in[d].astype(f32)).astype(bf16)
+        pix_copies.extend(over_z(d_y, d_sum, pix_sems.at[1], own_sems.at[6]))
+
+    gather_over_ch(g1, mid, tile, TILES, gn1, gf1, gh1, ready1, between)
+    late[0].wait()
+    for d in range(4):
+        r_y[d] = (r_mid[d, y].astype(f32) + r_in[d].astype(f32)).astype(bf16)
+    pix_copies += over_z(r_y, r_sum, pix_sems.at[2], own_sems.at[7])
 
     for i in range(PHASES):
         at = slice(i * 128, (i + 1) * 128)
@@ -1457,7 +1559,7 @@
 
     def gathered(parts):
         value = parts[0].astype(f32)
-        for d in range(1, PHASES):
+        for d in range(1, parts.shape[0]):
             value = value + parts[d].astype(f32)
         return value
 
@@ -1466,19 +1568,18 @@
     dilated_grad[...] = gathered(d_sum)
     for copy in zcopies:
         copy.wait()
-    del zown
 
 
 def run_backward(cid, arrays):
-    (grads, trunk, other, weight, norm3, masked, valid, expand, affine3, norm2, affine2, full2, taps, dilated,
-     norm1, affine1, reduce_rows, stats1, stats2, stats3) = arrays
+    (grads, trunk, others, weight, norm3, masked, valid, expand, affine3, norm2, affine2, full2, taps, dilated,
+     norm1, affine1, reduce_rows, stats1, stats2, stats3, picks, inputs) = arrays
     pixels, n = norm3.shape
     m = weight.shape[4]
     mid = norm2.shape[1]
     all_mid = SPLIT * mid
     outs = [
         shape((pixels, n), bf16),
-        shape((4, 27, 32, n), bf16),
+        shape((2, 27, 32, n), bf16),
         shape((all_mid // PHASES, 9 * mid), f32),
         shape((mid, 256), f32),
         shape((256, mid), f32),
@@ -1493,19 +1594,19 @@
         pltpu.VMEM((pixels, m), f32),
         pltpu.VMEM((2, pixels, m), bf16),
         pltpu.VMEM((2, pixels, m), bf16),
-        pltpu.VMEM((2, pixels + 128, n), bf16),
-        pltpu.VMEM((2, 3, pixels, 128), bf16),
-        pltpu.VMEM((3, pixels, 128), bf16),
-        pltpu.VMEM((3, 384, 2 * pixels), bf16),
-        pltpu.VMEM((4, 27, 32, n), bf16),
-        pltpu.VMEM((8, 128), f32),
+        pltpu.VMEM((4, pixels + 128, n), bf16),
+        pltpu.VMEM((4, 256, mid), bf16),
+        pltpu.VMEM((3, 192, pixels), bf16),
+        pltpu.VMEM((3, 192, 4 * pixels), bf16),
+        pltpu.VMEM((2, 27, 32, n), bf16),
+        pltpu.VMEM((4, 256, mid), bf16),
         pltpu.VMEM((pixels, n), f32),
         pltpu.VMEM((pixels, n), bf16),
         *sums[:4],
         pltpu.VMEM((pixels, mid), f32),
         pltpu.VMEM((pixels, mid), f32),
         pltpu.VMEM((pixels, all_mid), bf16),
-        pltpu.VMEM((pixels, 9 * mid), f32),
+        pltpu.VMEM((pixels // ROW_CLASSES, 9 * mid), f32),
         pltpu.VMEM((4, PHASES, 32, mid), bf16),
         pltpu.VMEM((pixels, all_mid), bf16),
         pltpu.VMEM((8, 128), f32),
@@ -1516,16 +1617,19 @@
         pltpu.VMEM((PHASES, 8, 128), f32),
         pltpu.VMEM((SPLIT, mid, n), bf16),
         pltpu.VMEM((SPLIT, mid, n), bf16),
-        pltpu.VMEM((PHASES, mid, 256), bf16),
-        pltpu.VMEM((PHASES, all_mid // PHASES, 9 * mid), bf16),
-        pltpu.VMEM((PHASES, all_mid // PHASES, 9 * mid), bf16),
-        pltpu.VMEM((SPLIT, n, mid), bf16),
-        pltpu.VMEM((SPLIT * n, mid), bf16),
-        pltpu.VMEM((PHASES, 256, mid), bf16),
+        pltpu.VMEM((4, mid, 256), bf16),
+        pltpu.VMEM((4, mid, 256), bf16),
+        pltpu.VMEM((4, mid, 256), bf16),
+        pltpu.VMEM((2, 4, all_mid // PHASES, 9 * mid), bf16),
+        pltpu.VMEM((4, all_mid // PHASES, 9 * mid), bf16),
+        pltpu.VMEM((4, all_mid // PHASES, 9 * mid), bf16),
+        pltpu.VMEM((4, all_mid // PHASES, 9 * mid), bf16),
+        pltpu.VMEM((4, 2, 256, mid), bf16),
+        pltpu.VMEM((4, 256, mid), bf16),
         dma(9, 3),
         dma(2, 2, PHASES),
-        dma(2),
-        dma(2, 4),
+        dma(3, 4),
+        dma(2, 27),
         dma(1, 2, TILES, 2),
         dma(1, 2, TILES),
         dma(3, 2, PHASES),
@@ -1534,11 +1638,14 @@
         dma(2, 2),
         dma(2, 2, SPLIT),
         dma(3, 2, PHASES),
+        dma(2, 3),
+        dma(8),
+        dma(2),
         dma(8),
     ]
     vmem = pl.BlockSpec(memory_space=pltpu.VMEM)
     specs = [vmem] * len(arrays)
-    specs[3] = pl.BlockSpec(memory_space=pl.ANY)
+    specs[1] = specs[2] = specs[3] = specs[12] = specs[21] = pl.BlockSpec(memory_space=pl.ANY)
     return pl.pallas_call(
         backward,
         out_shape=outs,
@@ -1553,20 +1660,19 @@
 
 
 def finish_pyramid(parts, result):
-    value = parts[0, 0].astype(f32)
-    for i in range(1, 4):
-        value = value + parts[i, 0].astype(f32)
-    result[0] = value.T
+    for i in range(parts.shape[1]):
+        result[i] = (parts[0, i].astype(f32) + parts[1, i].astype(f32)).T
 
 
 def run_finish(parts):
     steps, n = parts.shape[1], parts.shape[3]
+    each = 9
     return pl.pallas_call(
         finish_pyramid,
-        grid=(steps,),
+        grid=(steps // each,),
         out_shape=shape((steps, n, 32), f32),
-        in_specs=[pl.BlockSpec((4, 1, 32, n), lambda i: (0, i, 0, 0))],
-        out_specs=pl.BlockSpec((1, n, 32), lambda i: (i, 0, 0)),
+        in_specs=[pl.BlockSpec((2, each, 32, n), lambda i: (0, i, 0, 0))],
+        out_specs=pl.BlockSpec((each, n, 32), lambda i: (i, 0, 0)),
         name="finish_pyramid",
     )(parts)
 
@@ -1647,10 +1753,10 @@
     norm_two, act_two_full, taps_one, stat_two = run_stage_two(
         2, padded_one, valid_wide, dilated_weight.reshape(9 * local_mid, full_mid), affine(dilated_gain, dilated_bias)
     )
-    norm_three, trunk_class, stat_three = run_stage_three(
+    norm_three, trunk_class, stat_three, inputs_all = run_stage_three(
         3, act_two_full, expand_cols, masked, valid_wide, affine(expand_gain, expand_bias)
     )
-    grad_full, predictions, head_grad, branch_sums, trunk_other = run_pyramid(
+    grad_full, predictions, head_grad, branch_sums, trunk_other, picks = run_pyramid(
         4, trunk_class, aspp_weight, heads_all[32:40], head_weight, target_class, square_all
     )
     predictions = from_classes(predictions.transpose(0, 2, 1), rows_here, width)[:, :, :outs_count]
@@ -1666,7 +1772,7 @@
         [
             grad_full, trunk_class, trunk_other, aspp_weight, norm_three, masked, valid_wide, expand_cols,
             affine(expand_gain, expand_bias), norm_two, affine(dilated_gain, dilated_bias), act_two_full, taps_one,
-            dilated_rows, norm_one, affine(reduce_gain, reduce_bias), reduce_rows, stat_one, stat_two, stat_three,
+            dilated_rows, norm_one, affine(reduce_gain, reduce_bias), reduce_rows, stat_one, stat_two, stat_three, picks, inputs_all,
         ],
     )
     features_grad = features_grad.reshape(rows_here, width, local_in)

time: 422 us -> 336 us (0.80)
  Pallas kernels: 384 us -> 298 us
    pallas_call x1, Pallas kernels: 211 us -> 125 us  [run_backward(): pl.pallas_call(backward, out_shape=outs, in_specs=specs, out_specs=[vmem,...]
    pallas_call x1, Pallas kernels: 52.8 us -> 65 us  [run_pyramid(): pl.pallas_call(pyramid, out_shape=outs, in_specs=specs, out_specs=[vmem]...]
    pallas_call x4, Pallas kernels: 120 us -> 108 us  [the longest x3 103 us: call(): pl.pallas_call(kernel, out_shape=outs, in_specs=[hbm if i in hbm_ins else...]
where the time goes in v2:
time: 336 us; the launch traced here: 330 us
  Pallas kernels  298 us (89%)
  local copies, waits for them, and re-layouts  25.1 us (7%)
  other arithmetic  4.68 us (1%)
    pallas_call x1, Pallas kernels, run_backward(): pl.pallas_call(backward, out_shape=outs, in_specs=specs, out_specs=[vmem,...  125 us
    pallas_call x3, Pallas kernels, call(): pl.pallas_call(kernel, out_shape=outs, in_specs=[hbm if i in hbm_ins else...  103 us
    pallas_call x1, Pallas kernels, run_pyramid(): pl.pallas_call(pyramid, out_shape=outs, in_specs=specs, out_specs=[vmem]...  65 us
    unnamed x24, local copies, waits for them, and re-layouts  11 us

profile of v2, /device:TPU:0, one launch (start us, length us, event | category | flops | bytes accessed | tf_op | source)
XLA Modules:
  0.0 329.7 jit_solution(704677453872419896)
XLA Ops:
  0.6 0.7 convert_element_type.8
  1.3 0.1 reshape_reshape.9
  1.5 0.1 copy.50
  1.6 0.1 broadcast_in_dim.40
  1.7 1.0 broadcast_in_dim.41.valid
  2.7 0.1 pad.22.clone
  2.8 1.4 maximum_maximum_fusion.2
  4.1 0.7 convert_bitcast_fusion
  4.9 0.1 reshape.115
  5.0 0.8 reshape.101
  5.7 0.8 reshape.102
  6.5 0.2 concatenate.23
  6.7 0.6 pad.9.heads
  7.3 0.1 mul.18
  7.4 0.2 slice.54
  7.6 1.1 copy.52
  8.7 0.1 copy.53
  8.7 0.2 broadcast_multiply_fusion
  9.0 0.1 pad.18.clone
  9.0 1.0 pad_maximum_fusion.targets
  10.0 0.5 copy.55
  10.5 0.3 reshape_reshape.11
  10.8 0.2 fusion
  11.1 0.6 pad.10.square
  11.7 0.0 copy-start.6
  11.7 0.0 copy-start.7
  11.7 38.1 %stage_one.1 = (bf16[1024,512]{1,0:T(8,128)(2,1)}, bf16[512,512]{1,0:T(8,128)(2,1)}, bf16[512,512]{1,0:T(8,128)(2,1)}, f32[4,40,256]{2,1,0:T(8,128)}, f32[8,128,...) custom-call(bf16[1024,512]{1,0:T(8,128)(2,1)} %bitcast.65, ...), custom_call_target="tpu_custom_call" | custom-call | tf_op jit(solution)/shard_map/stage_one/pallas_call | solution.py:341
  49.8 0.0 copy-start.1
  49.8 27.9 %stage_two.1 = (f32[1024,128]{1,0:T(8,128)}, bf16[1024,512]{1,0:T(8,128)(2,1)}, bf16[1024,1152]{1,0:T(8,128)(2,1)}, f32[8,128]{1,0:T(8,128)}) custom-call(bf16[8,6,32,128]{3,2,1,0:T(8,128)(2,1)} %get-tuple-element.46.padded, f32[1024,128]{1,0:T(8,128)} %broadcast_in_dim.41.valid, bf16[1152,512]{1,0:T(8,128)(2,1)} %bitcast.57, ...), custom_call_target="tpu_custom_call" | custom-call | tf_op jit(solution)/shard_map/stage_two/pallas_call | solution.py:341
  77.7 0.0 copy-done.6
  77.7 0.0 copy-done.7
  77.7 0.7 maximum_maximum_fusion.affine.affine3
  78.4 37.1 %stage_three.1 = (f32[1024,512]{1,0:T(8,128)}, bf16[1024,512]{1,0:T(8,128)(2,1)}, f32[8,512]{1,0:T(8,128)}, bf16[4,1024,512]{2,1,0:T(8,128)(2,1)}) custom-call(bf16[1024,512]{1,0:T(8,128)(2,1)} %get-tuple-element.47.full.full2, bf16[512,512]{1,0:T(8,128)(2,1)} %get-tuple-element.48.weight.expand, bf16[1024,512]{1,0:T(8,128)(2,1)} %get-tuple-element.49.masked, ...), custom_call_target="tpu_custom_call" | custom-call | tf_op jit(solution)/shard_map/stage_three/pallas_call | solution.py:341
  115.5 0.0 copy-done.1
  115.5 0.1 reshape.105
  115.7 0.7 slice.57.affine
  116.5 0.1 copy.57
  116.6 0.8 slice.59.heads
  117.4 65.0 %pyramid.1 = (bf16[1024,768]{1,0:T(8,128)(2,1)}, f32[8,32,128]{2,1,0:T(8,128)}, f32[32,768]{1,0:T(8,128)}, f32[8,256]{1,0:T(8,128)}, bf16[3,1024,512]{2,1,0:T(8,128)(2,1)}, /*index=5*/bf16[3,192,256]{2,1,0:T(8,128)(2,1)}) custom-call(bf16[1024,512]{1,0:T(8,128)(2,1)} %get-tuple-element.50.trunk, bf16[3,3,3,512,256]{4,3,2,1,0:T(8,128)(2,1)} %weight.5, ...), custom_call_target="tpu_custom_call" | custom-call | tf_op jit(solution)/shard_map/pyramid/pallas_call | solution.py:1147
  182.4 1.2 reshape.107
  183.6 0.3 copy.58
  183.9 0.8 copy.60
  184.7 124.9 %backward.1 = (bf16[1024,512]{1,0:T(8,128)(2,1)}, bf16[2,27,32,512]{3,2,1,0:T(8,128)(2,1)}, f32[64,1152]{1,0:T(8,128)}, f32[128,256]{1,0:T(8,128)}, f32[256,128]...) custom-call(bf16[1024,768]{1,0:T(8,128)(2,1)} %get-tuple-element.55.grads, ...), custom_call_target="tpu_custom_call" | custom-call | tf_op jit(solution)/shard_map/backward/pallas_call | solution.py:1649
  309.7 1.3 slice_bitcast_fusion
  310.9 1.1 reshape.110
  312.0 0.7 copy.61
  312.8 1.4 fusion.3
  314.1 5.4 %finish_pyramid.1 = f32[27,512,32]{2,1,0:T(8,128)} custom-call(bf16[2,27,32,512]{3,2,1,0:T(8,128)(2,1)} %get-tuple-element.74.parts), custom_call_target="tpu_custom_call" | custom-call | tf_op jit(solution)/shard_map/finish_pyramid/pallas_call | solution.py:1670
  319.5 0.0 copy-start.5
  319.5 0.0 copy-start.4
  319.5 0.0 copy-start
  319.5 6.0 %copy.62 = f32[3,3,3,512,32]{3,4,2,1,0:T(8,128)} copy(f32[3,3,3,512,32]{4,3,2,1,0:T(8,128)} %bitcast.56) | data formatting | bytes 3538944
  325.5 0.0 copy-start.3
  325.5 0.0 copy-done.5
  325.5 0.7 dynamic-slice_bitcast_fusion
  326.2 0.0 copy-done.4
  326.2 0.1 reshape.113
  326.4 0.6 slice.74
  327.0 0.0 copy-done
  327.0 1.0 copy.69
  328.0 0.0 copy-done.3
  328.0 0.7 copy.70
  328.6 0.0 copy-done.2
  328.6 0.7 copy.71
  (13 shorter events, 0.2 us)
Async XLA Ops:
  11.7 66.0 %copy-start.6 = (f32[512]{0:T(512)S(1)}, f32[512]{0:T(512)}, u32[]{:S(2)}) copy-start(f32[512]{0:T(512)} %param.26) | copy-start | bytes 6148
  11.7 66.0 %copy-start.7 = (f32[512]{0:T(512)S(1)}, f32[512]{0:T(512)}, u32[]{:S(2)}) copy-start(f32[512]{0:T(512)} %param.25) | copy-start | bytes 6148
  49.8 65.7 %copy-start.1 = (f32[4,40,256]{2,1,0:T(8,128)S(1)}, f32[4,40,256]{2,1,0:T(8,128)}, u32[]{:S(2)}) copy-start(f32[4,40,256]{2,1,0:T(8,128)} %get-tuple-element.51) | copy-start | bytes 491524
  319.5 6.0 %copy-start.5 = (f32[8,256]{1,0:T(8,128)S(1)}, f32[8,256]{1,0:T(8,128)}, u32[]{:S(2)}) copy-start(f32[8,256]{1,0:T(8,128)} %get-tuple-element.75) | copy-start | bytes 24580
  319.5 6.7 %copy-start.4 = (f32[32,768]{1,0:T(8,128)S(1)}, f32[32,768]{1,0:T(8,128)}, u32[]{:S(2)}) copy-start(f32[32,768]{1,0:T(8,128)} %get-tuple-element.76) | copy-start | bytes 294916
  319.5 7.5 %copy-start = (bf16[1024,512]{1,0:T(8,128)(2,1)S(1)}, bf16[1024,512]{1,0:T(8,128)(2,1)}, u32[]{:S(2)}) copy-start(bf16[1024,512]{1,0:T(8,128)(2,1)} %get-tuple-element.67) | copy-start | bytes 3145732
  325.5 2.5 copy-start.3
  325.5 3.1 copy-start.2
